TPU v7x, 128 devices: a whole 4x4x4 slice. The times are simulated.
128 devices in a mesh: det: 4 (over x), tm: 32 (over y, z, core).
Axes of the slice: x: 4, y: 4, z: 4, core: 2. Of those that a mesh axis runs over, the one named last changes fastest.
Arguments:
- samples: float32 [4, 32, 128, 256], P('det', 'tm')
- pointing: int32 [4, 32, 128, 256], P('det', 'tm'), may hold values from 0 to 16383, as said below
- angles: float32 [4, 32, 128, 256], P('det', 'tm'), may hold values from -3.1415927 to 3.1415927
- counts: int32 [4, 32, 128], P('det', 'tm'), may hold values from 1 to 256, as said below
- sky_map: float32 [3, 256, 8192], P(None, ('det', 'tm'))
- prior_precision: float32 [3, 256, 4096], P(None, 'det', 'tm'), may hold values from 0.5 to 5
- omega_noise: float32 [6, 256, 4096], P(None, 'det', 'tm'), may hold values from -6 to 6
- omega_prior: float32 [6, 256, 4096], P(None, 'det', 'tm'), may hold values from -6 to 6
Outputs:
- gains: float32 [4, 32], P('det', 'tm')
- binned: float32 [3, 256, 8192], P(None, ('det', 'tm'))
- solution: float32 [6, 256, 4096], P(None, 'det', 'tm')
Inputs may be any that keep to these rules, and one draw needn't show every extreme that they name: The first counts[g, t, k] slots of a row hold samples; some sky tile takes 256 samples from every device, and every device fills at least one tile. `pointing`: pixel within the destination tile, cycle-major with 8192 pixels a cycle.
All inputs are finite; a program needn't handle non-finite values.
Results may differ from a plain program's by a relative error of at most 0.0003.
Values sent between devices are 32-bit elements; how exact they have to be, the bound alone decides.
A program may use at most 128 MiB of HBM per device.

v0:
```python
import math

import jax
import jax.numpy as jnp
from jax import lax
from jax.sharding import PartitionSpec as P

ITERS = 3


def with_halo(cells, sides, width):
    for axis, dim in sides:
        count = lax.axis_size(axis)
        ends = count - 1
        head = lax.slice_in_dim(cells, 0, width, axis=dim)
        tail = lax.slice_in_dim(cells, cells.shape[dim] - width, cells.shape[dim], axis=dim)
        cells = jnp.concatenate(
            [
                lax.ppermute(tail, axis, [(i, (i + 1) % count) for i in range(ends)]),
                cells,
                lax.ppermute(head, axis, [((i + 1) % count, i) for i in range(ends)]),
            ],
            axis=dim,
        )
    return cells


def cycle_modes(field):
    nphi = field.shape[-1]
    cycles = field.shape[1]
    second = 128
    first = nphi // second
    half = second // 2
    highest = lax.Precision.HIGHEST
    values = field.reshape(3, cycles, first, second)
    row_a = lax.broadcasted_iota(jnp.int32, (first, first), 0)
    col_a = lax.broadcasted_iota(jnp.int32, (first, first), 1)
    angle_a = 2.0 * math.pi / first * (row_a * col_a % first).astype(jnp.float32)
    cos_a = jnp.cos(angle_a)
    sin_a = jnp.sin(angle_a)
    real_y = jnp.einsum("kj,crjb->crkb", cos_a, values, precision=highest)
    imag_y = -jnp.einsum("kj,crjb->crkb", sin_a, values, precision=highest)
    row_t = lax.broadcasted_iota(jnp.int32, (first, second), 0)
    col_t = lax.broadcasted_iota(jnp.int32, (first, second), 1)
    angle_t = 2.0 * math.pi / nphi * (row_t * col_t % nphi).astype(jnp.float32)
    cos_t = jnp.cos(angle_t)
    sin_t = jnp.sin(angle_t)
    real_z = real_y * cos_t + imag_y * sin_t
    imag_z = imag_y * cos_t - real_y * sin_t
    row_b = lax.broadcasted_iota(jnp.int32, (half, second), 0)
    col_b = lax.broadcasted_iota(jnp.int32, (half, second), 1)
    angle_b = 2.0 * math.pi / second * (row_b * col_b % second).astype(jnp.float32)
    cos_b = jnp.cos(angle_b)
    sin_b = jnp.sin(angle_b)
    real_x = jnp.einsum("qj,crkj->crqk", cos_b, real_z, precision=highest) + jnp.einsum(
        "qj,crkj->crqk", sin_b, imag_z, precision=highest
    )
    imag_x = jnp.einsum("qj,crkj->crqk", cos_b, imag_z, precision=highest) - jnp.einsum(
        "qj,crkj->crqk", sin_b, real_z, precision=highest
    )
    scale = 1.0 / math.sqrt(nphi)
    real_x = real_x.reshape(3, cycles, half * first) * scale
    imag_x = imag_x.reshape(3, cycles, half * first) * scale
    return jnp.stack([real_x, imag_x], axis=1).reshape(6, cycles, half * first)


def operate(field, root, diagonal):
    scaled = root * field
    padded = with_halo(scaled, (("det", 1),), 1)
    beside = padded[:, 2:] + padded[:, :-2]
    return diagonal * field - 0.45 * root * beside


def squares(vector):
    return lax.psum(jnp.sum(vector * vector), ("det", "tm"))


def per_device(
    samples, pointing, angles, counts, sky_map, prior_precision, omega_noise, omega_prior
):
    tiles = samples.shape[2]
    slots_cap = samples.shape[3]
    n_tm = lax.axis_size("tm")
    rdev = sky_map.shape[1]
    nphi = sky_map.shape[2]
    pixels = rdev * nphi
    flat_data = samples.reshape(tiles, slots_cap)
    flat_angle = angles.reshape(tiles, slots_cap)
    flat_pixel = pointing.reshape(tiles, slots_cap).astype(jnp.float32)
    flat_count = counts.reshape(tiles, 1).astype(jnp.float32)
    got_data, got_angle, got_pixel, got_count = (
        lax.all_to_all(flat_data, ("det", "tm"), split_axis=0, concat_axis=0, tiled=True),
        lax.all_to_all(flat_angle, ("det", "tm"), split_axis=0, concat_axis=0, tiled=True),
        lax.all_to_all(flat_pixel, ("det", "tm"), split_axis=0, concat_axis=0, tiled=True),
        lax.all_to_all(flat_count, ("det", "tm"), split_axis=0, concat_axis=0, tiled=True),
    )
    pixel_index = got_pixel.astype(jnp.int32)
    slot_index = lax.broadcasted_iota(jnp.int32, (tiles, slots_cap), 1).astype(jnp.float32)
    valid = (slot_index < got_count).astype(jnp.float32)
    sky_flat = sky_map.reshape(3, pixels)
    cosine = jnp.cos(2.0 * got_angle)
    sine = jnp.sin(2.0 * got_angle)
    looked = sky_flat[:, pixel_index]
    signal = looked[0] + looked[1] * cosine + looked[2] * sine
    masked_signal = valid * signal
    part_cross = jnp.sum(masked_signal * got_data, axis=1)
    part_square = jnp.sum(masked_signal * signal, axis=1)
    total_cross, total_square = lax.psum((part_cross, part_square), ("det", "tm"))
    gains_all = total_cross / (total_square + 1e-06)
    position = lax.axis_index("det") * n_tm + lax.axis_index("tm")
    own_gain = lax.dynamic_slice_in_dim(gains_all, position, 1).reshape(1, 1)
    residual = valid * (got_data - gains_all[:, None] * signal)
    weights = jnp.stack([residual, residual * cosine, residual * sine]).reshape(3, -1)
    binned = jnp.zeros((3, pixels), jnp.float32).at[:, pixel_index.reshape(-1)].add(weights)
    cycle_index = (pixel_index // nphi).reshape(1, -1)
    cycle_ids = lax.broadcasted_iota(jnp.int32, (rdev, 1), 0)
    hits = jnp.sum(jnp.where(cycle_index == cycle_ids, valid.reshape(1, -1), 0.0), axis=1)
    binned = binned.reshape(3, rdev, nphi)
    planes = cycle_modes(binned)
    modes_count = planes.shape[2]
    weight_plane = jnp.broadcast_to((hits / nphi)[None, :, None], (1, rdev, modes_count))
    spectrum, weight = (
        lax.all_to_all(planes, "tm", split_axis=2, concat_axis=1, tiled=True),
        lax.all_to_all(weight_plane, "tm", split_axis=2, concat_axis=1, tiled=True),
    )
    precision = jnp.repeat(prior_precision, 2, axis=0)
    root = jnp.sqrt(precision)
    diagonal = precision + weight
    rhs = spectrum + jnp.sqrt(weight) * omega_noise + root * omega_prior
    solution = jnp.zeros_like(rhs)
    resid = rhs
    direction = rhs
    norm_now = squares(resid)
    for iteration in range(ITERS):
        image = operate(direction, root, diagonal)
        alpha = norm_now / lax.psum(jnp.sum(direction * image), ("det", "tm"))
        solution = solution + alpha * direction
        resid = resid - alpha * image
        norm_next = squares(resid)
        direction = resid + norm_next / norm_now * direction
        norm_now = norm_next
    return (own_gain, binned, solution)


def solution(mesh):
    return jax.shard_map(
        per_device,
        mesh=mesh,
        in_specs=(
            P("det", "tm", None, None),
            P("det", "tm", None, None),
            P("det", "tm", None, None),
            P("det", "tm", None),
            P(None, ("det", "tm"), None),
            P(None, "det", "tm"),
            P(None, "det", "tm"),
            P(None, "det", "tm"),
        ),
        out_specs=(P("det", "tm"), P(None, ("det", "tm"), None), P(None, "det", "tm")),
        check_vma=False,
    )
```

profile of v0, /device:TPU:1, one launch (start us, length us, event | category | flops | bytes accessed | tf_op | source)
XLA Modules:
  0.0 916.2 jit_solution(12387809444874937302)
XLA Ops:
  2.1 11.5 %all-to-all-start = ((f32[128,1,1]{2,1,0:T(1,128)}), f32[128,1,1]{2,1,0:T(1,128)S(1)}, u32[]{:S(2)}, u32[]{:S(2)}) async-start(f32[128,1,1]{2,1,0:T(1,128)} %copy.94), calls=%async_computation | async-start | bytes 131072 | tf_op jit(solution)/shard_map/all_to_all | solution.py:95
  17.1 5.5 copy.95
  23.3 9.8 %all-to-all-start.1 = ((f32[128,1,256]{2,1,0:T(1,128)}), f32[128,1,256]{2,1,0:T(1,128)S(1)}, u32[]{:S(2)}, u32[]{:S(2)}) async-start(f32[128,1,256]{2,1,0:T(1,128)} %bitcast.185), calls=%async_computation.1 | async-start | bytes 262144 | tf_op jit(solution)/shard_map/all_to_all | solution.py:94
  34.3 8.5 all-to-all-done.1
  42.9 4.5 all-to-all-start.2
  47.6 111.6 %gather_fusion = f32[32768,3]{1,0:T(8,128)} fusion(f32[3,16384]{0,1:T(8,128)} %bitcast.192, s32[32768]{0:T(1024)S(1)} %broadcast_clamp_fusion), kind=kCustom, calls=%fused_computation | custom fusion | bytes 917504 | tf_op jit(solution)/shard_map/gather | solution.py:103
  159.1 12.8 %slice.70 = f32[1,128,256]{0,2,1:T(8,128)} slice(f32[3,128,256]{0,2,1:T(8,128)} %bitcast.188), slice={[2:3], [0:128], [0:256]} | slice | bytes 262144 | tf_op jit(solution)/shard_map/slice | solution.py:104
  171.9 9.9 %copy.117 = f32[1,128,256]{2,1,0:T(8,128)S(1)} copy(f32[1,128,256]{0,2,1:T(8,128)} %slice.70) | data formatting | bytes 262144
  181.8 9.5 %copy.120 = f32[1,128,256]{2,0,1:T(1,128)S(1)} copy(f32[1,128,256]{0,2,1:T(8,128)} %slice.70) | data formatting | bytes 262144
  191.3 10.0 %copy.97 = f32[128,256,3]{1,0,2:T(8,128)S(1)} copy(f32[128,256,3]{2,1,0:T(8,128)} %bitcast.189) | data formatting | bytes 786432 | tf_op jit(solution)/shard_map/gather | solution.py:103
  201.3 9.8 %all-to-all-start.3 = ((f32[128,1,256]{2,1,0:T(1,128)}), f32[128,1,256]{2,1,0:T(1,128)S(1)}, u32[]{:S(2)}, u32[]{:S(2)}) async-start(f32[128,1,256]{2,1,0:T(1,128)} %all_to_all.54), calls=%async_computation.3 | async-start | bytes 262144 | tf_op jit(solution)/shard_map/all_to_all | solution.py:92
  215.0 5.8 all-to-all-done.3
  221.4 63.1 %all-reduce.1 = (f32[128]{0:T(128)S(1)}, f32[128]{0:T(128)S(1)}) all-reduce(f32[128]{0:T(128)S(1)} %get-tuple-element.27, f32[128]{0:T(128)S(1)} %get-tuple-element.26), channel_id=1, replica_groups=mesh['det'=4,'tm'=32] {'det','tm'}, use_global_device_ids=true, to_apply=%region_1.0 | all-reduce | flops 256 | bytes 2048 | tf_op jit(solution)/shard_map/psum | solution.py:108
  284.5 4.3 reshape_multiply_fusion
  292.7 8.6 copy.102
  301.5 178.1 %scatter_custom_fusion = f32[3,16384]{0,1:T(8,128)} fusion(s32[32768]{0:T(1024)S(1)} %bitcast.214, f32[32768,3]{1,0:T(8,128)} %copy.102, f32[]{:T(128)} %constant.71.clone.1), kind=kCustom, calls=%fused_computation.2 | custom fusion | flops 98304 | bytes 197120 | tf_op jit(solution)/shard_map/scatter-add | solution.py:114
  479.7 5.2 copy.103
  490.3 19.4 %reduce.2 = f32[4096,2]{1,0:T(8,128)} reduce(f32[4096,1,2]{2,1,0:T(1,128)S(1)} %broadcast_bitcast_fusion, f32[]{:T(128)} %broadcast.332), dimensions={1}, to_apply=%broadcast_bitcast_fusion.reduce_sub_computation | reduce | bytes 65540
  513.3 5.1 all-to-all-start.5
  518.5 4.4 copy.108
  523.0 8.7 reshape.363
  531.6 7.4 all-to-all-start.4
  548.5 7.9 reshape.364
  556.3 5.2 copy.109
  563.0 4.0 collective-permute-start.1
  568.5 63.5 %all-reduce = (f32[]{:T(128)}, f32[]{:T(128)}) all-reduce(f32[]{:T(128)} %get-tuple-element.25, f32[]{:T(128)} %get-tuple-element.24), channel_id=1, replica_groups=mesh['det'=4,'tm'=32] {'det','tm'}, use_global_device_ids=true, to_apply=%region_7.8 | all-reduce | flops 2 | bytes 16 | tf_op jit(solution)/shard_map/psum | solution.py:75
  634.0 63.5 %psum.60 = f32[]{:T(128)} all-reduce(f32[]{:T(128)} %multiply_reduce_fusion.2), channel_id=1, replica_groups=mesh['det'=4,'tm'=32] {'det','tm'}, use_global_device_ids=true, to_apply=%region_11.12 | all-reduce | flops 1 | bytes 8 | tf_op jit(solution)/shard_map/psum | solution.py:75
  700.3 4.0 collective-permute-start.3
  705.8 64.2 %psum.61 = f32[]{:T(128)} all-reduce(f32[]{:T(128)} %multiply_reduce_fusion.1), channel_id=1, replica_groups=mesh['det'=4,'tm'=32] {'det','tm'}, use_global_device_ids=true, to_apply=%region_13.14 | all-reduce | flops 1 | bytes 8 | tf_op jit(solution)/shard_map/psum | solution.py:136
  772.1 64.2 %psum.62 = f32[]{:T(128)} all-reduce(f32[]{:T(128)} %multiply_reduce_fusion), channel_id=1, replica_groups=mesh['det'=4,'tm'=32] {'det','tm'}, use_global_device_ids=true, to_apply=%region_15.16 | all-reduce | flops 1 | bytes 8 | tf_op jit(solution)/shard_map/psum | solution.py:75
  843.2 5.9 copy.111
  850.5 63.1 %psum.63 = f32[]{:T(128)} all-reduce(f32[]{:T(128)} %fusion.23), channel_id=1, replica_groups=mesh['det'=4,'tm'=32] {'det','tm'}, use_global_device_ids=true, to_apply=%region_17.18 | all-reduce | flops 1 | bytes 8 | tf_op jit(solution)/shard_map/psum | solution.py:136
  (80 shorter events, 49.1 us)
Async XLA Ops:
  0.6 22.0 %copy-start.3 = (f32[1,1,128,256]{3,2,1,0:T(8,128)S(1)}, f32[1,1,128,256]{3,2,1,0:T(8,128)}, u32[]{:S(2)}) copy-start(f32[1,1,128,256]{3,2,1,0:T(8,128)} %param.8) | copy-start | bytes 393220
  2.1 21.3 %all-to-all-start = ((f32[128,1,1]{2,1,0:T(1,128)}), f32[128,1,1]{2,1,0:T(1,128)S(1)}, u32[]{:S(2)}, u32[]{:S(2)}) async-start(f32[128,1,1]{2,1,0:T(1,128)} %copy.94), calls=%async_computation | async-start | bytes 131072 | tf_op jit(solution)/shard_map/all_to_all | solution.py:95
  23.3 19.5 %all-to-all-start.1 = ((f32[128,1,256]{2,1,0:T(1,128)}), f32[128,1,256]{2,1,0:T(1,128)S(1)}, u32[]{:S(2)}, u32[]{:S(2)}) async-start(f32[128,1,256]{2,1,0:T(1,128)} %bitcast.185), calls=%async_computation.1 | async-start | bytes 262144 | tf_op jit(solution)/shard_map/all_to_all | solution.py:94
  42.9 158.5 %all-to-all-start.2 = ((f32[128,1,256]{2,1,0:T(1,128)}), f32[128,1,256]{2,1,0:T(1,128)S(1)}, u32[]{:S(2)}, u32[]{:S(2)}) async-start(f32[128,1,256]{2,1,0:T(1,128)} %all_to_all.52), calls=%async_computation.2 | async-start | bytes 262144 | tf_op jit(solution)/shard_map/all_to_all | solution.py:93
  201.3 19.5 %all-to-all-start.3 = ((f32[128,1,256]{2,1,0:T(1,128)}), f32[128,1,256]{2,1,0:T(1,128)S(1)}, u32[]{:S(2)}, u32[]{:S(2)}) async-start(f32[128,1,256]{2,1,0:T(1,128)} %all_to_all.54), calls=%async_computation.3 | async-start | bytes 262144 | tf_op jit(solution)/shard_map/all_to_all | solution.py:92
  513.3 18.3 %all-to-all-start.5 = ((f32[32,1,256]{2,1,0:T(1,128)}), f32[32,1,256]{2,1,0:T(1,128)S(1)}, u32[]{:S(2)}, u32[]{:S(2)}) async-start(f32[32,1,256]{2,1,0:T(1,128)} %reshape.365), calls=%async_computation.5 | async-start | bytes 65536 | tf_op jit(solution)/shard_map/all_to_all | solution.py:124
  523.0 38.6 %copy-start = (f32[3,64,128]{2,1,0:T(8,128)S(1)}, f32[3,64,128]{2,1,0:T(8,128)}, u32[]{:S(2)}) copy-start(f32[3,64,128]{2,1,0:T(8,128)} %param.13) | copy-start | bytes 294916
  523.0 38.6 %copy-start.1 = (f32[6,64,128]{2,1,0:T(8,128)S(1)}, f32[6,64,128]{2,1,0:T(8,128)}, u32[]{:S(2)}) copy-start(f32[6,64,128]{2,1,0:T(8,128)} %param.15) | copy-start | bytes 589828
  523.0 38.6 %copy-start.2 = (f32[6,64,128]{2,1,0:T(8,128)S(1)}, f32[6,64,128]{2,1,0:T(8,128)}, u32[]{:S(2)}) copy-start(f32[6,64,128]{2,1,0:T(8,128)} %param.14) | copy-start | bytes 589828
  531.6 15.7 %all-to-all-start.4 = ((f32[32,1,1536]{2,1,0:T(1,128)}), f32[32,1,1536]{2,1,0:T(1,128)S(1)}, u32[]{:S(2)}, u32[]{:S(2)}) async-start(f32[32,1,1536]{2,1,0:T(1,128)} %reshape.363), calls=%async_computation.4 | async-start | bytes 393216 | tf_op jit(solution)/shard_map/all_to_all | solution.py:123
  561.7 5.3 collective-permute-start
  563.0 4.7 collective-permute-start.1
  699.0 5.3 collective-permute-start.2
  700.3 4.7 collective-permute-start.3
  837.9 11.2 %collective-permute-start.4 = (f32[6,1,128]{2,1,0:T(1,128)S(1)}, f32[6,1,128]{2,1,0:T(1,128)S(1)}, u32[]{:S(2)}, u32[]{:S(2)}) collective-permute-start(f32[6,1,128]{2,1,0:T(1,128)S(1)} %get-tuple-element.40), channel_id=1, source_target_pairs={{32,0},{64,32},{96,64},{33,1},{65,33},{97,65},{34,2},{66,34},{98,6... | collective-permute-start | bytes 9224 | tf_op jit(solution)/shard_map/ppermute | solution.py:21
  839.2 9.9 %collective-permute-start.5 = (f32[6,1,128]{2,1,0:T(1,128)S(1)}, f32[6,1,128]{2,1,0:T(1,128)S(1)}, u32[]{:S(2)}, u32[]{:S(2)}) collective-permute-start(f32[6,1,128]{2,1,0:T(1,128)S(1)} %get-tuple-element.41), channel_id=1, source_target_pairs={{0,32},{32,64},{64,96},{1,33},{33,65},{65,97},{2,34},{34,66},{66,9... | collective-permute-start | bytes 9224 | tf_op jit(solution)/shard_map/ppermute | solution.py:19
where the time goes:
time: 925 us; the launch traced here: 916 us
  blocking collectives  382 us (41%)
  local copies, waits for them, and re-layouts  220 us (24%)
  other arithmetic  220 us (24%)
  starting transfers between devices  63.8 us (7%)
  waiting for transfers between devices  19.4 us (2%)
    psum x3, blocking collectives, squares(): return lax.psum(jnp.sum(vector * vector), ('det', 'tm'))  191 us
    scatter-add x1, other arithmetic, per_device(): jnp.zeros((3, pixels), jnp.float32).at[:, pixel_index.reshape(-1)]  178 us
    psum x2, blocking collectives, per_device(): alpha = norm_now / lax.psum(jnp.sum(direction * image), ('det', 'tm'))  127 us
    gather x2, local copies, waits for them, and re-layouts, per_device(): looked = sky_flat[:, pixel_index]  122 us
    psum x1, blocking collectives, per_device(): lax.psum((part_cross, part_square), ('det', 'tm'))  63.1 us
    unnamed x19, local copies, waits for them, and re-layouts  56.4 us
    unnamed x2, other arithmetic  19.5 us
  transfers between devices with their start and end apart: 12, of which 5 were waited for; matrix products, arithmetic and copies ran while one was open for 21% of the time, Pallas kernels for 0%

commit v1 on v0

v1 whole, which is shorter than its diff:
```python
import math

import jax
import jax.numpy as jnp
import numpy as np
from jax import lax
from jax.experimental import pallas as pl
from jax.experimental.pallas import tpu as pltpu
from jax.sharding import PartitionSpec as P

MESH = pl.DeviceIdType.MESH
HIGHEST = lax.Precision.HIGHEST
F32 = jnp.float32
BF16 = jnp.bfloat16
NDET = 4
NTM = 32
NDEV = NDET * NTM
GROUP = 16
NGROUP = NDEV // GROUP
UNROLL_G = 2
UNROLL_S = 2
SHIFT = 4.0
SCALE = 4.0
STEP_MAX = 20.0


def tables():
    h, i = np.divmod(np.arange(128), 64)
    a = 2 * i + h
    k = np.arange(128)
    ang = 2.0 * np.pi * (np.outer(a, k) % 128) / 128
    first = np.concatenate([np.cos(ang), -np.sin(ang)], axis=1)
    b = np.arange(64)
    ang = 2.0 * np.pi * np.outer(b, k) / 8192
    twist = np.stack([np.cos(ang), np.sin(ang)])
    q = np.arange(32)
    ang = 2.0 * np.pi * (np.outer(q, b) % 64) / 64
    c, s = np.cos(ang), np.sin(ang)
    last = np.concatenate([np.concatenate([c, s], axis=1), np.concatenate([-s, c], axis=1)], axis=0)
    last = last / math.sqrt(8192)
    return [np.asarray(x, np.float32) for x in (first, twist, last)]


def one_hot(row, rows):
    value = jnp.broadcast_to(row, (16, 128)).astype(BF16)
    index = lax.broadcasted_iota(jnp.int32, (rows, 128), 0).astype(F32).astype(BF16)
    same = index.reshape(rows // 16, 16, 128) == value[None]
    return jnp.where(same, jnp.ones((), BF16), jnp.zeros((), BF16)).reshape(rows, 128)


def kernel(
    samples, pointing, angles, counts, sky, prec, onoise, oprior, first, twist, last,
    gain_out, map_out, sol_out,
    sbuf, rbuf, table, hi_s, lo_s, cos_s, sin_s, look, wsplit, acc,
    stat_r, spec_s, spec_r, pp, bw, v1_s, v2_s, mom_r,
    send_sem, recv_sem, stat_send, stat_recv, spec_send, spec_recv,
    edge_send, edge_recv, mom_send, mom_recv,
):
    det = lax.axis_index("det")
    tm = lax.axis_index("tm")
    me = det * NTM + tm

    def place(p):
        return (p // NTM, p % NTM)

    barrier = pltpu.get_barrier_semaphore()

    @pl.loop(1, NDEV)
    def _(o):
        pl.semaphore_signal(barrier, inc=1, device_id=place((me + o) % NDEV), device_id_type=MESH)

    row_i = lax.broadcasted_iota(jnp.int32, (128, 128), 0)
    col_i = lax.broadcasted_iota(jnp.int32, (128, 128), 1)
    for half in range(2):
        lanes = slice(half * 128, half * 128 + 128)
        sbuf[pl.ds(half, 128, stride=8), :] = samples[:, lanes]
        sbuf[pl.ds(2 + half, 128, stride=8), :] = angles[:, lanes]
        sbuf[pl.ds(4 + half, 128, stride=8), :] = pointing[:, lanes].astype(F32)
    count_row = jnp.broadcast_to(counts[...].astype(F32), (128, 128))
    count_col = jnp.sum(jnp.where(row_i == col_i, count_row, 0.0), axis=1, keepdims=True)
    count_full = jnp.broadcast_to(count_col, (128, 128))
    sbuf[pl.ds(6, 128, stride=8), :] = count_full
    sbuf[pl.ds(7, 128, stride=8), :] = count_full

    for c in range(3):
        blocks = []
        for cyc in range(2):
            turned = sky[c, pl.ds(cyc, 64, stride=2), :].T
            blocks.append(jnp.concatenate([turned[:64], turned[64:]], axis=1))
        full = jnp.concatenate(blocks, axis=1)
        upper = full.astype(BF16)
        table[pl.ds(c * 64, 64), :] = upper
        table[pl.ds(192 + c * 64, 64), :] = (full - upper.astype(F32)).astype(BF16)

    pp[:, 8:72, :] = prec[...]

    @pl.when(det == 0)
    def _():
        pp[:, 0:8, :] = jnp.zeros((3, 8, 128), F32)
        bw[:, 0:8, :] = jnp.zeros((7, 8, 128), F32)

    @pl.when(det == NDET - 1)
    def _():
        pp[:, 72:80, :] = jnp.zeros((3, 8, 128), F32)
        bw[:, 72:80, :] = jnp.zeros((7, 8, 128), F32)

    acc[...] = jnp.zeros_like(acc)
    pl.semaphore_wait(barrier, NDEV - 1)

    my_group = me // GROUP

    @pl.loop(1, NDEV)
    def _(o):
        to = (me + o) % NDEV
        pltpu.make_async_remote_copy(
            sbuf.at[pl.ds(to * 8, 8)], rbuf.at[pl.ds(me * 8, 8)],
            send_sem, recv_sem.at[my_group], device_id=place(to), device_id_type=MESH,
        ).start()

    def edge_copy(src, dst, index, where):
        return pltpu.make_async_remote_copy(
            src, dst, edge_send.at[index], edge_recv.at[index], device_id=where, device_id_type=MESH
        )

    prec_down = edge_copy(prec.at[:, 56:64, :], pp.at[:, 0:8, :], 0, ((det + 1) % NDET, tm))
    prec_up = edge_copy(prec.at[:, 0:8, :], pp.at[:, 72:80, :], 1, ((det + NDET - 1) % NDET, tm))

    @pl.when(det < NDET - 1)
    def _():
        prec_down.start()

    @pl.when(det > 0)
    def _():
        prec_up.start()

    rbuf[pl.ds(me * 8, 8), :] = sbuf[pl.ds(me * 8, 8), :]

    col_index = lax.broadcasted_iota(jnp.int32, (64, 128), 0).astype(F32)

    def gather_group(group):
        base = group * GROUP
        for half in range(2):
            pixel = rbuf[pl.ds(base * 8 + 4 + half, GROUP, stride=8), :].astype(jnp.int32)
            upper = (pixel >> 13) * 128 + ((pixel >> 6) & 1) * 64 + ((pixel >> 7) & 63)
            hi_s[half, pl.ds(base, GROUP), :] = upper.astype(F32)
            lo_s[half, pl.ds(base, GROUP), :] = (pixel & 63).astype(F32)

        @pl.loop(0, GROUP // UNROLL_G)
        def _(step):
            for u in range(UNROLL_G):
                s = base + step * UNROLL_G + u
                hots = [one_hot(hi_s[half, pl.ds(s, 1), :], 256) for half in range(2)]
                got = jnp.dot(table[...], jnp.concatenate(hots, axis=1), preferred_element_type=F32)
                got = got[:192] + got[192:]
                for half in range(2):
                    low = lo_s[half, pl.ds(s, 1), :]
                    same = col_index == low
                    for c in range(3):
                        part = got[c * 64 : c * 64 + 64, half * 128 : half * 128 + 128]
                        look[c, half, pl.ds(s, 1), :] = jnp.sum(
                            jnp.where(same, part, 0.0), axis=0, keepdims=True
                        )

    @pl.loop(0, NGROUP)
    def _(t):
        group = (my_group + t) % NGROUP

        @pl.when(t == 0)
        def _():
            span = rbuf.at[pl.ds(0, (GROUP - 1) * 8)]
            pltpu.make_async_copy(span, span, recv_sem.at[my_group]).wait()

        @pl.when(t > 0)
        def _():
            span = rbuf.at[pl.ds(0, GROUP * 8)]
            pltpu.make_async_copy(span, span, recv_sem.at[group]).wait()

        gather_group(group)

    count = rbuf[pl.ds(6, 128, stride=8), :]
    slot = col_i.astype(F32)
    cross = jnp.zeros((128, 128), F32)
    square = jnp.zeros((128, 128), F32)
    for half in range(2):
        angle = rbuf[pl.ds(2 + half, 128, stride=8), :]
        cosine = jnp.cos(2.0 * angle)
        sine = jnp.sin(2.0 * angle)
        cos_s[half] = cosine
        sin_s[half] = sine
        signal = look[0, half] + look[1, half] * cosine + look[2, half] * sine
        look[0, half] = signal
        masked = jnp.where(slot + 128.0 * half < count, signal, 0.0)
        cross = cross + masked * rbuf[pl.ds(half, 128, stride=8), :]
        square = square + masked * signal
    cross = jnp.sum(cross.T, axis=0, keepdims=True)
    square = jnp.sum(square.T, axis=0, keepdims=True)
    stat_r[me] = jnp.concatenate([cross, square], axis=0)

    @pl.loop(1, NDEV)
    def _(o):
        pltpu.make_async_remote_copy(
            stat_r.at[me], stat_r.at[me], stat_send, stat_recv,
            device_id=place((me + o) % NDEV), device_id_type=MESH,
        ).start()

    rest = stat_r.at[pl.ds(0, NDEV - 1)]
    pltpu.make_async_copy(rest, rest, stat_recv).wait()
    total = jnp.sum(stat_r[...], axis=0)
    gains = total[0:1] / (total[1:2] + 1e-06)
    lane = lax.broadcasted_iota(jnp.int32, (1, 128), 1)
    gain_out[...] = jnp.sum(jnp.where(lane == me, gains, 0.0), axis=1, keepdims=True)
    gain_full = jnp.broadcast_to(gains, (128, 128)).T

    hits = [jnp.zeros((1, 128), F32) for _ in range(2)]
    for half in range(2):
        data = rbuf[pl.ds(half, 128, stride=8), :]
        good = slot + 128.0 * half < count
        residual = jnp.where(good, data - gain_full * look[0, half], 0.0)
        for c, weight in enumerate((residual, residual * cos_s[half], residual * sin_s[half])):
            upper = weight.astype(BF16).astype(F32)
            wsplit[c, half] = upper
            wsplit[3 + c, half] = weight - upper
        late = jnp.where(hi_s[half] >= 128.0, 1.0, 0.0)
        valid = jnp.where(good, 1.0, 0.0)
        hits[1] = hits[1] + jnp.sum(valid * late, axis=0, keepdims=True)
        hits[0] = hits[0] + jnp.sum(valid * (1.0 - late), axis=0, keepdims=True)

    low_index = lax.broadcasted_iota(jnp.int32, (64, 128), 0).astype(F32).astype(BF16).reshape(4, 16, 128)

    @pl.loop(0, NDEV // UNROLL_S)
    def _(step):
        lefts = []
        rights = []
        for u in range(UNROLL_S):
            s = step * UNROLL_S + u
            for half in range(2):
                rights.append(one_hot(hi_s[half, pl.ds(s, 1), :], 256))
                low = jnp.broadcast_to(lo_s[half, pl.ds(s, 1), :], (16, 128)).astype(BF16)
                same = low_index == low[None]
                rows = []
                for w in range(6):
                    value = jnp.broadcast_to(wsplit[w, half, pl.ds(s, 1), :], (16, 128)).astype(BF16)
                    rows.append(jnp.where(same, value[None], jnp.zeros((), BF16)).reshape(64, 128))
                lefts.append(jnp.concatenate(rows, axis=0))
        acc[...] += lax.dot_general(
            jnp.concatenate(lefts, axis=1), jnp.concatenate(rights, axis=1),
            (((1,), (1,)), ((), ())), preferred_element_type=F32,
        )

    field = acc[:192] + acc[192:]

    z_parts = []
    for cyc in range(2):
        y = jnp.dot(
            field[:, cyc * 128 : cyc * 128 + 128], first[...],
            precision=HIGHEST, preferred_element_type=F32,
        )
        for c in range(3):
            y_re = y[c * 64 : c * 64 + 64, :128]
            y_im = y[c * 64 : c * 64 + 64, 128:]
            z_re = y_re * twist[0] + y_im * twist[1]
            z_im = y_im * twist[0] - y_re * twist[1]
            z_parts.append(jnp.concatenate([z_re, z_im], axis=0))
    x = jnp.dot(
        last[...], jnp.concatenate(z_parts, axis=1), precision=HIGHEST, preferred_element_type=F32
    )
    for cyc in range(2):
        for c in range(3):
            block = x[:, (cyc * 3 + c) * 128 : (cyc * 3 + c) * 128 + 128]
            spec_s[pl.ds(4 * c + cyc, 32, stride=16), :] = block[:32]
            spec_s[pl.ds(4 * c + 2 + cyc, 32, stride=16), :] = block[32:]
        weight = jnp.sum(hits[cyc], axis=1, keepdims=True) * (1.0 / 8192)
        spec_s[pl.ds(12 + cyc, 32, stride=16), :] = jnp.broadcast_to(weight, (32, 128))
        spec_s[pl.ds(14 + cyc, 32, stride=16), :] = jnp.broadcast_to(weight, (32, 128))

    @pl.loop(1, NTM)
    def _(o):
        to = (tm + o) % NTM
        pltpu.make_async_remote_copy(
            spec_s.at[pl.ds(to * 16, 16)], spec_r.at[pl.ds(tm * 16, 16)],
            spec_send, spec_recv, device_id=(det, to), device_id_type=MESH,
        ).start()

    spec_r[pl.ds(tm * 16, 16), :] = spec_s[pl.ds(tm * 16, 16), :]
    for c in range(3):
        for cyc in range(2):
            part = field[c * 64 : c * 64 + 64, cyc * 128 : cyc * 128 + 128]
            part = jnp.concatenate([part[:, :64], part[:, 64:]], axis=0)
            map_out[c, pl.ds(cyc, 64, stride=2), :] = part.T

    span = spec_r.at[pl.ds(0, (NTM - 1) * 16)]
    pltpu.make_async_copy(span, span, spec_recv).wait()

    for cyc in range(2):
        for j in range(7):
            bw[j, pl.ds(8 + cyc, 32, stride=2), :] = spec_r[pl.ds(2 * j + cyc, 32, stride=16), :]
    noise_root = jnp.sqrt(bw[6, 8:72, :])
    for c in range(3):
        root = jnp.sqrt(prec[c])
        for p in range(2):
            j = 2 * c + p
            bw[j, 8:72, :] = bw[j, 8:72, :] + noise_root * onoise[j] + root * oprior[j]
    rhs_down = edge_copy(bw.at[:, 64:72, :], bw.at[:, 0:8, :], 2, ((det + 1) % NDET, tm))
    rhs_up = edge_copy(bw.at[:, 8:16, :], bw.at[:, 72:80, :], 3, ((det + NDET - 1) % NDET, tm))

    @pl.when(det < NDET - 1)
    def _():
        rhs_down.start()

    @pl.when(det > 0)
    def _():
        rhs_up.start()

    @pl.when(det > 0)
    def _():
        prec_down.wait_recv()
        rhs_down.wait_recv()

    @pl.when(det < NDET - 1)
    def _():
        prec_up.wait_recv()
        rhs_up.wait_recv()

    moments = [jnp.zeros((8, 128), F32) for _ in range(6)]
    for c in range(3):
        precision = pp[c]
        root = jnp.sqrt(precision)
        side = root * (0.45 / SCALE)
        diagonal = (precision + bw[6] - SHIFT) * (1.0 / SCALE)

        def step(v):
            u = root * v
            beside = pltpu.roll(u, 1, 0) + pltpu.roll(u, 79, 0)
            return diagonal * v - side * beside

        for p in range(2):
            j = 2 * c + p
            v0 = bw[j]
            v1 = step(v0)
            v2 = step(v1)
            v3 = step(v2)
            own = [v[8:72] for v in (v0, v1, v2, v3)]
            v1_s[j] = own[1]
            v2_s[j] = own[2]
            for m, (a, b) in enumerate(((0, 0), (0, 1), (1, 1), (1, 2), (2, 2), (2, 3))):
                moments[m] = moments[m] + jnp.sum((own[a] * own[b]).reshape(8, 8, 128), axis=0)
    message = jnp.zeros((1, 128), F32)
    for m in range(6):
        value = jnp.sum(jnp.sum(moments[m], axis=0, keepdims=True), axis=1, keepdims=True)
        message = jnp.where(lane == m, jnp.broadcast_to(value, (1, 128)), message)
    mom_r[me] = message

    @pl.loop(1, NDEV)
    def _(o):
        pltpu.make_async_remote_copy(
            mom_r.at[me], mom_r.at[me], mom_send, mom_recv,
            device_id=place((me + o) % NDEV), device_id_type=MESH,
        ).start()

    rest = mom_r.at[pl.ds(0, NDEV - 1)]
    pltpu.make_async_copy(rest, rest, mom_recv).wait()
    sums = jnp.sum(mom_r[...], axis=0)
    nu = [jnp.sum(jnp.where(lane == m, sums, 0.0), axis=1, keepdims=True) for m in range(6)]

    zero = jnp.zeros((1, 1), F32)

    def inner(a, b):
        terms = {}
        for i, x_i in enumerate(a):
            for j, y_j in enumerate(b):
                terms[i + j] = terms.get(i + j, zero) + x_i * y_j
        out = zero
        for power, value in terms.items():
            out = out + value * nu[power]
        return out

    def image_of(a):
        longer = list(a) + [zero]
        return [SHIFT * longer[i] + (SCALE * longer[i - 1] if i else zero) for i in range(len(longer))]

    resid = [zero + 1.0]
    direction = [zero + 1.0]
    answer = [zero, zero, zero]
    norm_now = nu[0]
    for iteration in range(3):
        image = image_of(direction)
        alpha = norm_now / inner(direction, image)
        alpha = jnp.minimum(jnp.maximum(alpha, 0.0), STEP_MAX)
        for i, value in enumerate(direction):
            answer[i] = answer[i] + alpha * value
        if iteration < 2:
            resid = resid + [zero]
            resid = [r - alpha * w for r, w in zip(resid, image)]
            norm_next = jnp.maximum(inner(resid, resid), 0.0)
            beta = norm_next / norm_now
            direction = [r + beta * d for r, d in zip(resid, direction + [zero])]
            norm_now = norm_next
    for j in range(6):
        sol_out[j] = answer[0] * bw[j, 8:72, :] + answer[1] * v1_s[j] + answer[2] * v2_s[j]

    span = sbuf.at[pl.ds(0, (NDEV - 1) * 8)]
    pltpu.make_async_copy(span, span, send_sem).wait()
    rest = stat_r.at[pl.ds(0, NDEV - 1)]
    pltpu.make_async_copy(rest, rest, stat_send).wait()
    span = spec_s.at[pl.ds(0, (NTM - 1) * 16)]
    pltpu.make_async_copy(span, span, spec_send).wait()
    rest = mom_r.at[pl.ds(0, NDEV - 1)]
    pltpu.make_async_copy(rest, rest, mom_send).wait()

    @pl.when(det < NDET - 1)
    def _():
        prec_down.wait_send()
        rhs_down.wait_send()

    @pl.when(det > 0)
    def _():
        prec_up.wait_send()
        rhs_up.wait_send()


def per_device(
    samples, pointing, angles, counts, sky_map, prior_precision, omega_noise, omega_prior
):
    sky = sky_map.reshape(3, 2, 64, 128).transpose(0, 2, 1, 3).reshape(3, 128, 128)
    vmem = pl.BlockSpec(memory_space=pltpu.VMEM)
    dma = pltpu.SemaphoreType.DMA
    gain, binned, solved = pl.pallas_call(
        kernel,
        name="gibbs_step",
        out_shape=(
            jax.ShapeDtypeStruct((1, 1), F32),
            jax.ShapeDtypeStruct((3, 128, 128), F32),
            jax.ShapeDtypeStruct((6, 64, 128), F32),
        ),
        in_specs=[vmem] * 11,
        out_specs=(vmem, vmem, vmem),
        scratch_shapes=[
            pltpu.VMEM((1024, 128), F32),
            pltpu.VMEM((1024, 128), F32),
            pltpu.VMEM((384, 256), BF16),
            pltpu.VMEM((2, 128, 128), F32),
            pltpu.VMEM((2, 128, 128), F32),
            pltpu.VMEM((2, 128, 128), F32),
            pltpu.VMEM((2, 128, 128), F32),
            pltpu.VMEM((3, 2, 128, 128), F32),
            pltpu.VMEM((6, 2, 128, 128), F32),
            pltpu.VMEM((384, 256), F32),
            pltpu.VMEM((NDEV, 2, 128), F32),
            pltpu.VMEM((NTM * 16, 128), F32),
            pltpu.VMEM((NTM * 16, 128), F32),
            pltpu.VMEM((3, 80, 128), F32),
            pltpu.VMEM((7, 80, 128), F32),
            pltpu.VMEM((6, 64, 128), F32),
            pltpu.VMEM((6, 64, 128), F32),
            pltpu.VMEM((NDEV, 1, 128), F32),
            dma, dma((NGROUP,)), dma, dma, dma, dma, dma((4,)), dma((4,)), dma, dma,
        ],
        compiler_params=pltpu.CompilerParams(collective_id=0, has_side_effects=True),
    )(
        samples.reshape(128, 256),
        pointing.reshape(128, 256),
        angles.reshape(128, 256),
        counts.reshape(1, 128),
        sky,
        prior_precision,
        omega_noise,
        omega_prior,
        *(jnp.asarray(t) for t in tables()),
    )
    binned = binned.reshape(3, 64, 2, 128).transpose(0, 2, 1, 3).reshape(3, 2, 8192)
    return (gain, binned, solved)


def solution(mesh):
    return jax.shard_map(
        per_device,
        mesh=mesh,
        in_specs=(
            P("det", "tm", None, None),
            P("det", "tm", None, None),
            P("det", "tm", None, None),
            P("det", "tm", None),
            P(None, ("det", "tm"), None),
            P(None, "det", "tm"),
            P(None, "det", "tm"),
            P(None, "det", "tm"),
        ),
        out_specs=(P("det", "tm"), P(None, ("det", "tm"), None), P(None, "det", "tm")),
        check_vma=False,
    )
```

time: 925 us -> 91.3 us (0.10)
  blocking collectives: 382 us -> 0 us
  other arithmetic: 220 us -> 0 us
  local copies, waits for them, and re-layouts: 220 us -> 2.34 us
  Pallas kernels: 0 us -> 86.3 us
  starting transfers between devices: 63.8 us -> 0 us
  waiting for transfers between devices: 19.4 us -> 0 us
    psum x6 -> x0, blocking collectives: 382 us -> none  [the longest x3 191 us: squares(): return lax.psum(jnp.sum(vector * vector), ('det', 'tm'))]
    scatter-add x1 -> x0, other arithmetic: 178 us -> none  [per_device(): jnp.zeros((3, pixels), jnp.float32).at[:, pixel_index.reshape(-1)]]
    gather x2 -> x0, local copies, waits for them, and re-layouts: 122 us -> none  [per_device(): looked = sky_flat[:, pixel_index]]
    pallas_call x0 -> x1, Pallas kernels: none -> 86.3 us  [per_device(): pl.pallas_call(kernel, name='gibbs_step', out_shape=(jax.ShapeDtypeStruct...]
    unnamed x19 -> x4, local copies, waits for them, and re-layouts: 56.4 us -> 2.34 us
    all_to_all x6 -> x0, starting transfers between devices: 48 us -> none  [the longest x1 11.5 us: per_device(): lax.all_to_all(flat_count, ('det', 'tm'), split_axis=0, concat_axis=0, ti...]
    unnamed x2 -> x0, other arithmetic: 19.5 us -> none
    all_to_all x6 -> x0, waiting for transfers between devices: 17.9 us -> none  [the longest x1 8.55 us: per_device(): lax.all_to_all(flat_pixel, ('det', 'tm'), split_axis=0, concat_axis=0, ti...]
  transfers between devices with their start and end apart: 12 -> 0, of which waited for: 5 -> 0; matrix products, arithmetic and copies ran while one was open for 21% -> 0% of each run, Pallas kernels for 0% -> 0%
where the time goes in v1:
time: 91.3 us; the launch traced here: 91.1 us
  Pallas kernels  86.3 us (95%)
  between operations  2.47 us (3%)
  local copies, waits for them, and re-layouts  2.34 us (3%)
    pallas_call x1, Pallas kernels, per_device(): pl.pallas_call(kernel, name='gibbs_step', out_shape=(jax.ShapeDtypeStruct...  86.3 us
    unnamed x4, local copies, waits for them, and re-layouts  2.34 us

profile of v1, /device:TPU:1, one launch (start us, length us, event | category | flops | bytes accessed | tf_op | source)
XLA Modules:
  0.0 91.1 jit_solution(10776264175142614879)
XLA Ops:
  0.6 86.3 %gibbs_step.1 = (f32[1,1]{1,0:T(1,128)}, f32[3,128,128]{2,1,0:T(8,128)}, f32[6,64,128]{2,1,0:T(8,128)}) custom-call(f32[128,256]{1,0:T(8,128)} %bitcast.16, s32[128,256]{1,0:T(8,128)} %bitcast.17, f32[128,256]{1,0:T(8,128)} %bitcast.18, s32[1,128]{1,0:T(1,128)} %bitcast.19, f32[3,128,128]{2,1,0:T(8,128)} %bitcast.14, f32[3,64,128]{2,1,0:T(8,128)} %prec.1, ...), custom_call_target="tpu_custom_call" | custom-call | tf_op jit(solution)/shard_map/gibbs_step/pallas_call | solution.py:427
  87.6 0.0 copy-start
  87.6 1.7 %copy.20 = f32[3,2,8192]{2,1,0:T(2,128)} copy(f32[3,2,8192]{2,1,0:T(2,128)} %bitcast.15) | data formatting | bytes 393216
  89.3 0.0 copy-done
  89.3 0.7 copy.21
Async XLA Ops:
  87.6 1.7 %copy-start = (f32[6,64,128]{2,1,0:T(8,128)S(1)}, f32[6,64,128]{2,1,0:T(8,128)}, u32[]{:S(2)}) copy-start(f32[6,64,128]{2,1,0:T(8,128)} %get-tuple-element.14) | copy-start | bytes 589828

commit v2 on v1

--- a/solution.py
+++ b/solution.py
@@ -9,7 +9,6 @@
 from jax.sharding import PartitionSpec as P
 
 MESH = pl.DeviceIdType.MESH
-HIGHEST = lax.Precision.HIGHEST
 F32 = jnp.float32
 BF16 = jnp.bfloat16
 NDET = 4
@@ -17,8 +16,7 @@
 NDEV = NDET * NTM
 GROUP = 16
 NGROUP = NDEV // GROUP
-UNROLL_G = 2
-UNROLL_S = 2
+UNROLL = 16
 SHIFT = 4.0
 SCALE = 4.0
 STEP_MAX = 20.0
@@ -38,7 +36,39 @@
     c, s = np.cos(ang), np.sin(ang)
     last = np.concatenate([np.concatenate([c, s], axis=1), np.concatenate([-s, c], axis=1)], axis=0)
     last = last / math.sqrt(8192)
-    return [np.asarray(x, np.float32) for x in (first, twist, last)]
+    def split(x):
+        upper = x.astype(np.float32).astype(jnp.bfloat16)
+        return np.stack([upper, (x - upper.astype(np.float64)).astype(jnp.bfloat16)])
+
+    return [split(first), twist.astype(np.float32), split(last)]
+
+
+def split_parts(x):
+    upper = x.astype(BF16)
+    return upper, (x - upper.astype(F32)).astype(BF16)
+
+
+def dot3(a, b):
+    out = jnp.dot(a[0], b[0], preferred_element_type=F32)
+    out = out + jnp.dot(a[0], b[1], preferred_element_type=F32)
+    return out + jnp.dot(a[1], b[0], preferred_element_type=F32)
+
+
+def sine_cosine(x):
+    k = jnp.floor(x * (2.0 / math.pi) + 0.5)
+    r = ((x - k * 1.5703125) - k * 4.837512969970703125e-4) - k * 7.549789948768648e-8
+    z = r * r
+    sine = r + r * z * (-1.6666654611e-1 + z * (8.3321608736e-3 - z * 1.9515295891e-4))
+    cosine = 1.0 - 0.5 * z + z * z * (
+        4.166664568298827e-2 + z * (-1.388731625493765e-3 + z * 2.443315711809948e-5)
+    )
+    q = k.astype(jnp.int32) & 3
+    odd = (q & 1) == 1
+    s = jnp.where(odd, cosine, sine)
+    c = jnp.where(odd, sine, cosine)
+    s = jnp.where(q >= 2, -s, s)
+    c = jnp.where((q == 1) | (q == 2), -c, c)
+    return s, c
 
 
 def one_hot(row, rows):
@@ -51,23 +81,37 @@
 def kernel(
     samples, pointing, angles, counts, sky, prec, onoise, oprior, first, twist, last,
     gain_out, map_out, sol_out,
-    sbuf, rbuf, table, hi_s, lo_s, cos_s, sin_s, look, wsplit, acc,
-    stat_r, spec_s, spec_r, pp, bw, v1_s, v2_s, mom_r,
+    sbuf, rbuf, table, hi_s, lo_s, cos_s, sin_s, look, sums_s, wsplit, acc,
+    stat_r, spec_s, spec_r, pp, root_s, edge, bw, v1_s, v2_s, mom_r,
     send_sem, recv_sem, stat_send, stat_recv, spec_send, spec_recv,
-    edge_send, edge_recv, mom_send, mom_recv,
+    rim_send, rim_recv, edge_send, edge_recv, mom_send, mom_recv,
 ):
     det = lax.axis_index("det")
     tm = lax.axis_index("tm")
     me = det * NTM + tm
 
-    def place(p):
-        return (p // NTM, p % NTM)
+    ty, tz, tc = tm // 8, (tm // 2) % 4, tm % 2
+
+    def hop(d):
+        return jnp.where(d == 0, 2, jnp.where(d == 1, 1, jnp.where(d == 2, 3, 0)))
+
+    def other_tm(e):
+        y = (ty + hop(e // 8)) % 4
+        z = (tz + hop((e // 2) % 4)) % 4
+        return y * 8 + z * 2 + (tc + 1 - e % 2) % 2
+
+    def to_all(act):
+        @pl.loop(0, NTM - 1)
+        def _(e):
+            to = other_tm(e)
+            for x in (2, 1, 3, 0):
+                act(((det + x) % NDET, to))
+
+        for x in (2, 1, 3):
+            act(((det + x) % NDET, tm))
 
     barrier = pltpu.get_barrier_semaphore()
-
-    @pl.loop(1, NDEV)
-    def _(o):
-        pl.semaphore_signal(barrier, inc=1, device_id=place((me + o) % NDEV), device_id_type=MESH)
+    to_all(lambda to: pl.semaphore_signal(barrier, inc=1, device_id=to, device_id_type=MESH))
 
     row_i = lax.broadcasted_iota(jnp.int32, (128, 128), 0)
     col_i = lax.broadcasted_iota(jnp.int32, (128, 128), 1)
@@ -93,62 +137,97 @@
         table[pl.ds(192 + c * 64, 64), :] = (full - upper.astype(F32)).astype(BF16)
 
     pp[:, 8:72, :] = prec[...]
+    bw[:, 0:8, :] = jnp.zeros((7, 8, 128), F32)
+    bw[:, 72:80, :] = jnp.zeros((7, 8, 128), F32)
 
     @pl.when(det == 0)
     def _():
         pp[:, 0:8, :] = jnp.zeros((3, 8, 128), F32)
-        bw[:, 0:8, :] = jnp.zeros((7, 8, 128), F32)
+        edge[0] = jnp.zeros((12, 8, 128), F32)
+        spec_r[0:32, :] = jnp.zeros((32, 128), F32)
 
     @pl.when(det == NDET - 1)
     def _():
         pp[:, 72:80, :] = jnp.zeros((3, 8, 128), F32)
-        bw[:, 72:80, :] = jnp.zeros((7, 8, 128), F32)
+        edge[1] = jnp.zeros((12, 8, 128), F32)
+        spec_r[34 * 16 : 36 * 16, :] = jnp.zeros((32, 128), F32)
 
     acc[...] = jnp.zeros_like(acc)
     pl.semaphore_wait(barrier, NDEV - 1)
 
     my_group = me // GROUP
-
-    @pl.loop(1, NDEV)
-    def _(o):
-        to = (me + o) % NDEV
+    my_slot = me % GROUP
+    my_tile = rbuf.at[pl.ds(me * 8, 8)]
+
+    def send_samples(group, v):
+        slot = (my_slot + v) % GROUP
         pltpu.make_async_remote_copy(
-            sbuf.at[pl.ds(to * 8, 8)], rbuf.at[pl.ds(me * 8, 8)],
-            send_sem, recv_sem.at[my_group], device_id=place(to), device_id_type=MESH,
+            sbuf.at[pl.ds((group * GROUP + slot) * 8, 8)], my_tile, send_sem, recv_sem.at[my_group],
+            device_id=(group // 2, (group % 2) * GROUP + slot), device_id_type=MESH,
         ).start()
 
-    def edge_copy(src, dst, index, where):
-        return pltpu.make_async_remote_copy(
-            src, dst, edge_send.at[index], edge_recv.at[index], device_id=where, device_id_type=MESH
+    for v in range(1, GROUP):
+        send_samples(my_group, v)
+
+    @pl.loop(1, NGROUP)
+    def _(t):
+        group = (my_group + NGROUP - t) % NGROUP
+        for v in range(GROUP):
+            send_samples(group, v)
+
+    rbuf[pl.ds(me * 8, 8), :] = sbuf[pl.ds(me * 8, 8), :]
+
+    down = ((det + 1) % NDET, tm)
+    up = ((det + NDET - 1) % NDET, tm)
+
+    def edge_copies(rows, side, padded, to):
+        pairs = (
+            (prec.at[:, rows, :], pp.at[:, padded, :]),
+            (onoise.at[:, rows, :], edge.at[side, 0:6]),
+            (oprior.at[:, rows, :], edge.at[side, 6:12]),
         )
-
-    prec_down = edge_copy(prec.at[:, 56:64, :], pp.at[:, 0:8, :], 0, ((det + 1) % NDET, tm))
-    prec_up = edge_copy(prec.at[:, 0:8, :], pp.at[:, 72:80, :], 1, ((det + NDET - 1) % NDET, tm))
+        return [
+            pltpu.make_async_remote_copy(
+                src, dst, edge_send.at[side, i], edge_recv.at[side, i], device_id=to, device_id_type=MESH
+            )
+            for i, (src, dst) in enumerate(pairs)
+        ]
+
+    go_down = edge_copies(slice(56, 64), 0, slice(0, 8), down)
+    go_up = edge_copies(slice(0, 8), 1, slice(72, 80), up)
 
     @pl.when(det < NDET - 1)
     def _():
-        prec_down.start()
+        for copy in go_down:
+            copy.start()
 
     @pl.when(det > 0)
     def _():
-        prec_up.start()
-
-    rbuf[pl.ds(me * 8, 8), :] = sbuf[pl.ds(me * 8, 8), :]
+        for copy in go_up:
+            copy.start()
 
     col_index = lax.broadcasted_iota(jnp.int32, (64, 128), 0).astype(F32)
+
+    slot_index = lax.broadcasted_iota(jnp.int32, (GROUP, 128), 1).astype(F32)
 
     def gather_group(group):
         base = group * GROUP
+        here = pl.ds(base, GROUP)
+
+        def row(r):
+            return rbuf[pl.ds(base * 8 + r, GROUP, stride=8), :]
+
         for half in range(2):
-            pixel = rbuf[pl.ds(base * 8 + 4 + half, GROUP, stride=8), :].astype(jnp.int32)
+            pixel = row(4 + half).astype(jnp.int32)
             upper = (pixel >> 13) * 128 + ((pixel >> 6) & 1) * 64 + ((pixel >> 7) & 63)
-            hi_s[half, pl.ds(base, GROUP), :] = upper.astype(F32)
-            lo_s[half, pl.ds(base, GROUP), :] = (pixel & 63).astype(F32)
-
-        @pl.loop(0, GROUP // UNROLL_G)
-        def _(step):
-            for u in range(UNROLL_G):
-                s = base + step * UNROLL_G + u
+            hi_s[half, here, :] = upper.astype(F32)
+            lo_s[half, here, :] = (pixel & 63).astype(F32)
+            sine, cosine = sine_cosine(2.0 * row(2 + half))
+            sin_s[half, here, :] = sine
+            cos_s[half, here, :] = cosine
+        for first_s in range(0, GROUP, UNROLL):
+            for u in range(UNROLL):
+                s = base + first_s + u
                 hots = [one_hot(hi_s[half, pl.ds(s, 1), :], 256) for half in range(2)]
                 got = jnp.dot(table[...], jnp.concatenate(hots, axis=1), preferred_element_type=F32)
                 got = got[:192] + got[192:]
@@ -160,6 +239,21 @@
                         look[c, half, pl.ds(s, 1), :] = jnp.sum(
                             jnp.where(same, part, 0.0), axis=0, keepdims=True
                         )
+        count = row(6)
+        cross = jnp.zeros((GROUP, 128), F32)
+        square = jnp.zeros((GROUP, 128), F32)
+        for half in range(2):
+            signal = (
+                look[0, half, here, :]
+                + look[1, half, here, :] * cos_s[half, here, :]
+                + look[2, half, here, :] * sin_s[half, here, :]
+            )
+            look[0, half, here, :] = signal
+            masked = jnp.where(slot_index + 128.0 * half < count, signal, 0.0)
+            cross = cross + masked * row(half)
+            square = square + masked * signal
+        sums_s[0, here, :] = cross
+        sums_s[1, here, :] = square
 
     @pl.loop(0, NGROUP)
     def _(t):
@@ -177,32 +271,17 @@
 
         gather_group(group)
 
+    cross = jnp.sum(sums_s[0].T, axis=0, keepdims=True)
+    square = jnp.sum(sums_s[1].T, axis=0, keepdims=True)
+    mine = stat_r.at[me]
+    mine[...] = jnp.concatenate([cross, square], axis=0)
+    to_all(
+        lambda to: pltpu.make_async_remote_copy(
+            mine, mine, stat_send, stat_recv, device_id=to, device_id_type=MESH
+        ).start()
+    )
     count = rbuf[pl.ds(6, 128, stride=8), :]
     slot = col_i.astype(F32)
-    cross = jnp.zeros((128, 128), F32)
-    square = jnp.zeros((128, 128), F32)
-    for half in range(2):
-        angle = rbuf[pl.ds(2 + half, 128, stride=8), :]
-        cosine = jnp.cos(2.0 * angle)
-        sine = jnp.sin(2.0 * angle)
-        cos_s[half] = cosine
-        sin_s[half] = sine
-        signal = look[0, half] + look[1, half] * cosine + look[2, half] * sine
-        look[0, half] = signal
-        masked = jnp.where(slot + 128.0 * half < count, signal, 0.0)
-        cross = cross + masked * rbuf[pl.ds(half, 128, stride=8), :]
-        square = square + masked * signal
-    cross = jnp.sum(cross.T, axis=0, keepdims=True)
-    square = jnp.sum(square.T, axis=0, keepdims=True)
-    stat_r[me] = jnp.concatenate([cross, square], axis=0)
-
-    @pl.loop(1, NDEV)
-    def _(o):
-        pltpu.make_async_remote_copy(
-            stat_r.at[me], stat_r.at[me], stat_send, stat_recv,
-            device_id=place((me + o) % NDEV), device_id_type=MESH,
-        ).start()
-
     rest = stat_r.at[pl.ds(0, NDEV - 1)]
     pltpu.make_async_copy(rest, rest, stat_recv).wait()
     total = jnp.sum(stat_r[...], axis=0)
@@ -227,12 +306,12 @@
 
     low_index = lax.broadcasted_iota(jnp.int32, (64, 128), 0).astype(F32).astype(BF16).reshape(4, 16, 128)
 
-    @pl.loop(0, NDEV // UNROLL_S)
+    @pl.loop(0, NDEV // UNROLL)
     def _(step):
         lefts = []
         rights = []
-        for u in range(UNROLL_S):
-            s = step * UNROLL_S + u
+        for u in range(UNROLL):
+            s = step * UNROLL + u
             for half in range(2):
                 rights.append(one_hot(hi_s[half, pl.ds(s, 1), :], 256))
                 low = jnp.broadcast_to(lo_s[half, pl.ds(s, 1), :], (16, 128)).astype(BF16)
@@ -251,19 +330,14 @@
 
     z_parts = []
     for cyc in range(2):
-        y = jnp.dot(
-            field[:, cyc * 128 : cyc * 128 + 128], first[...],
-            precision=HIGHEST, preferred_element_type=F32,
-        )
+        y = dot3(split_parts(field[:, cyc * 128 : cyc * 128 + 128]), (first[0], first[1]))
         for c in range(3):
             y_re = y[c * 64 : c * 64 + 64, :128]
             y_im = y[c * 64 : c * 64 + 64, 128:]
             z_re = y_re * twist[0] + y_im * twist[1]
             z_im = y_im * twist[0] - y_re * twist[1]
             z_parts.append(jnp.concatenate([z_re, z_im], axis=0))
-    x = jnp.dot(
-        last[...], jnp.concatenate(z_parts, axis=1), precision=HIGHEST, preferred_element_type=F32
-    )
+    x = dot3((last[0], last[1]), split_parts(jnp.concatenate(z_parts, axis=1)))
     for cyc in range(2):
         for c in range(3):
             block = x[:, (cyc * 3 + c) * 128 : (cyc * 3 + c) * 128 + 128]
@@ -273,58 +347,77 @@
         spec_s[pl.ds(12 + cyc, 32, stride=16), :] = jnp.broadcast_to(weight, (32, 128))
         spec_s[pl.ds(14 + cyc, 32, stride=16), :] = jnp.broadcast_to(weight, (32, 128))
 
-    @pl.loop(1, NTM)
-    def _(o):
-        to = (tm + o) % NTM
+    def send_spectrum(where, to, slot, send, recv):
         pltpu.make_async_remote_copy(
-            spec_s.at[pl.ds(to * 16, 16)], spec_r.at[pl.ds(tm * 16, 16)],
-            spec_send, spec_recv, device_id=(det, to), device_id_type=MESH,
+            spec_s.at[pl.ds(to * 16, 16)], spec_r.at[pl.ds(slot * 16, 16)],
+            send, recv, device_id=(where, to), device_id_type=MESH,
         ).start()
 
-    spec_r[pl.ds(tm * 16, 16), :] = spec_s[pl.ds(tm * 16, 16), :]
+    low_end = jnp.logical_and(tm < 2, det > 0)
+    high_end = jnp.logical_and(tm >= NTM - 2, det < NDET - 1)
+
+    @pl.when(low_end)
+    def _():
+        @pl.loop(0, NTM)
+        def _(e):
+            send_spectrum(det - 1, other_tm(e), 34 + tm, rim_send, rim_recv.at[1])
+
+    @pl.when(high_end)
+    def _():
+        @pl.loop(0, NTM)
+        def _(e):
+            send_spectrum(det + 1, other_tm(e), tm - (NTM - 2), rim_send, rim_recv.at[0])
+
+    @pl.loop(0, NTM - 1)
+    def _(e):
+        send_spectrum(det, other_tm(e), 2 + tm, spec_send, spec_recv)
+
+    spec_r[pl.ds((2 + tm) * 16, 16), :] = spec_s[pl.ds(tm * 16, 16), :]
     for c in range(3):
         for cyc in range(2):
             part = field[c * 64 : c * 64 + 64, cyc * 128 : cyc * 128 + 128]
             part = jnp.concatenate([part[:, :64], part[:, 64:]], axis=0)
             map_out[c, pl.ds(cyc, 64, stride=2), :] = part.T
 
+    @pl.when(det > 0)
+    def _():
+        for copy in go_down:
+            copy.wait_recv()
+
+    @pl.when(det < NDET - 1)
+    def _():
+        for copy in go_up:
+            copy.wait_recv()
+
+    for c in range(3):
+        root_s[c] = jnp.sqrt(pp[c])
+
+    @pl.when(det > 0)
+    def _():
+        span = spec_r.at[pl.ds(0, 32)]
+        pltpu.make_async_copy(span, span, rim_recv.at[0]).wait()
+
+    @pl.when(det < NDET - 1)
+    def _():
+        span = spec_r.at[pl.ds(0, 32)]
+        pltpu.make_async_copy(span, span, rim_recv.at[1]).wait()
+
     span = spec_r.at[pl.ds(0, (NTM - 1) * 16)]
     pltpu.make_async_copy(span, span, spec_recv).wait()
 
     for cyc in range(2):
         for j in range(7):
-            bw[j, pl.ds(8 + cyc, 32, stride=2), :] = spec_r[pl.ds(2 * j + cyc, 32, stride=16), :]
-    noise_root = jnp.sqrt(bw[6, 8:72, :])
-    for c in range(3):
-        root = jnp.sqrt(prec[c])
-        for p in range(2):
-            j = 2 * c + p
-            bw[j, 8:72, :] = bw[j, 8:72, :] + noise_root * onoise[j] + root * oprior[j]
-    rhs_down = edge_copy(bw.at[:, 64:72, :], bw.at[:, 0:8, :], 2, ((det + 1) % NDET, tm))
-    rhs_up = edge_copy(bw.at[:, 8:16, :], bw.at[:, 72:80, :], 3, ((det + NDET - 1) % NDET, tm))
-
-    @pl.when(det < NDET - 1)
-    def _():
-        rhs_down.start()
-
-    @pl.when(det > 0)
-    def _():
-        rhs_up.start()
-
-    @pl.when(det > 0)
-    def _():
-        prec_down.wait_recv()
-        rhs_down.wait_recv()
-
-    @pl.when(det < NDET - 1)
-    def _():
-        prec_up.wait_recv()
-        rhs_up.wait_recv()
+            bw[j, pl.ds(4 + cyc, 36, stride=2), :] = spec_r[pl.ds(2 * j + cyc, 36, stride=16), :]
+    noise_root = jnp.sqrt(bw[6])
+    for j in range(6):
+        noise = jnp.concatenate([edge[0, j], onoise[j], edge[1, j]], axis=0)
+        prior = jnp.concatenate([edge[0, 6 + j], oprior[j], edge[1, 6 + j]], axis=0)
+        bw[j] = bw[j] + noise_root * noise + root_s[j // 2] * prior
 
     moments = [jnp.zeros((8, 128), F32) for _ in range(6)]
     for c in range(3):
         precision = pp[c]
-        root = jnp.sqrt(precision)
+        root = root_s[c]
         side = root * (0.45 / SCALE)
         diagonal = (precision + bw[6] - SHIFT) * (1.0 / SCALE)
 
@@ -348,15 +441,13 @@
     for m in range(6):
         value = jnp.sum(jnp.sum(moments[m], axis=0, keepdims=True), axis=1, keepdims=True)
         message = jnp.where(lane == m, jnp.broadcast_to(value, (1, 128)), message)
-    mom_r[me] = message
-
-    @pl.loop(1, NDEV)
-    def _(o):
-        pltpu.make_async_remote_copy(
-            mom_r.at[me], mom_r.at[me], mom_send, mom_recv,
-            device_id=place((me + o) % NDEV), device_id_type=MESH,
+    own_row = mom_r.at[me]
+    own_row[...] = message
+    to_all(
+        lambda to: pltpu.make_async_remote_copy(
+            own_row, own_row, mom_send, mom_recv, device_id=to, device_id_type=MESH
         ).start()
-
+    )
     rest = mom_r.at[pl.ds(0, NDEV - 1)]
     pltpu.make_async_copy(rest, rest, mom_recv).wait()
     sums = jnp.sum(mom_r[...], axis=0)
@@ -407,15 +498,20 @@
     rest = mom_r.at[pl.ds(0, NDEV - 1)]
     pltpu.make_async_copy(rest, rest, mom_send).wait()
 
+    @pl.when(jnp.logical_or(low_end, high_end))
+    def _():
+        span = spec_s.at[pl.ds(0, NTM * 16)]
+        pltpu.make_async_copy(span, span, rim_send).wait()
+
     @pl.when(det < NDET - 1)
     def _():
-        prec_down.wait_send()
-        rhs_down.wait_send()
+        for copy in go_down:
+            copy.wait_send()
 
     @pl.when(det > 0)
     def _():
-        prec_up.wait_send()
-        rhs_up.wait_send()
+        for copy in go_up:
+            copy.wait_send()
 
 
 def per_device(
@@ -443,17 +539,21 @@
             pltpu.VMEM((2, 128, 128), F32),
             pltpu.VMEM((2, 128, 128), F32),
             pltpu.VMEM((3, 2, 128, 128), F32),
+            pltpu.VMEM((2, 128, 128), F32),
             pltpu.VMEM((6, 2, 128, 128), F32),
             pltpu.VMEM((384, 256), F32),
             pltpu.VMEM((NDEV, 2, 128), F32),
             pltpu.VMEM((NTM * 16, 128), F32),
-            pltpu.VMEM((NTM * 16, 128), F32),
+            pltpu.VMEM(((NTM + 4) * 16, 128), F32),
             pltpu.VMEM((3, 80, 128), F32),
+            pltpu.VMEM((3, 80, 128), F32),
+            pltpu.VMEM((2, 12, 8, 128), F32),
             pltpu.VMEM((7, 80, 128), F32),
             pltpu.VMEM((6, 64, 128), F32),
             pltpu.VMEM((6, 64, 128), F32),
             pltpu.VMEM((NDEV, 1, 128), F32),
-            dma, dma((NGROUP,)), dma, dma, dma, dma, dma((4,)), dma((4,)), dma, dma,
+            dma, dma((NGROUP,)), dma, dma, dma, dma,
+            dma, dma((2,)), dma((2, 3)), dma((2, 3)), dma, dma,
         ],
         compiler_params=pltpu.CompilerParams(collective_id=0, has_side_effects=True),
     )(

time: 91.3 us -> 64.3 us (0.70)
  Pallas kernels: 86.3 us -> 59.3 us
    pallas_call x1, Pallas kernels: 86.3 us -> 59.3 us  [per_device(): pl.pallas_call(kernel, name='gibbs_step', out_shape=(jax.ShapeDtypeStruct...]
where the time goes in v2:
time: 64.3 us; the launch traced here: 64.1 us
  Pallas kernels  59.3 us (92%)
  between operations  2.47 us (4%)
  local copies, waits for them, and re-layouts  2.34 us (4%)
    pallas_call x1, Pallas kernels, per_device(): pl.pallas_call(kernel, name='gibbs_step', out_shape=(jax.ShapeDtypeStruct...  59.3 us
    unnamed x4, local copies, waits for them, and re-layouts  2.34 us

profile of v2, /device:TPU:1, one launch (start us, length us, event | category | flops | bytes accessed | tf_op | source)
XLA Modules:
  0.0 64.1 jit_solution(5521683375763080389)
XLA Ops:
  0.6 59.3 %gibbs_step.1 = (f32[1,1]{1,0:T(1,128)}, f32[3,128,128]{2,1,0:T(8,128)}, f32[6,64,128]{2,1,0:T(8,128)}) custom-call(f32[128,256]{1,0:T(8,128)} %bitcast.16, s32[128,256]{1,0:T(8,128)} %bitcast.17, f32[128,256]{1,0:T(8,128)} %bitcast.18, s32[1,128]{1,0:T(1,128)} %bitcast.19, f32[3,128,128]{2,1,0:T(8,128)} %bitcast.14, f32[3,64,128]{2,1,0:T(8,128)} %prec.1, ...), custom_call_target="tpu_custom_call" | custom-call | tf_op jit(solution)/shard_map/gibbs_step/pallas_call | solution.py:523
  60.6 0.0 copy-start
  60.6 1.7 %copy.20 = f32[3,2,8192]{2,1,0:T(2,128)} copy(f32[3,2,8192]{2,1,0:T(2,128)} %bitcast.15) | data formatting | bytes 393216
  62.3 0.0 copy-done
  62.3 0.7 %copy.21 = f32[6,64,128]{2,1,0:T(8,128)} copy(f32[6,64,128]{2,1,0:T(8,128)S(1)} %copy-done) | data formatting | bytes 393216
Async XLA Ops:
  60.6 1.7 %copy-start = (f32[6,64,128]{2,1,0:T(8,128)S(1)}, f32[6,64,128]{2,1,0:T(8,128)}, u32[]{:S(2)}) copy-start(f32[6,64,128]{2,1,0:T(8,128)} %get-tuple-element.14) | copy-start | bytes 589828

commit v3 on v2

--- a/solution.py
+++ b/solution.py
@@ -79,39 +79,58 @@
 
 
 def kernel(
-    samples, pointing, angles, counts, sky, prec, onoise, oprior, first, twist, last,
-    gain_out, map_out, sol_out,
+    samples_in, pointing_in, angles_in, counts_in, sky_in, prec, onoise_in, oprior_in,
+    first_in, twist_in, last_in,
+    gain_out, map_upper_out, map_lower_out, sol_out,
+    samples, pointing, angles, counts, sky, onoise, oprior, first, twist, last, map_s, sol_s,
     sbuf, rbuf, table, hi_s, lo_s, cos_s, sin_s, look, sums_s, wsplit, acc,
     stat_r, spec_s, spec_r, pp, root_s, edge, bw, v1_s, v2_s, mom_r,
     send_sem, recv_sem, stat_send, stat_recv, spec_send, spec_recv,
-    rim_send, rim_recv, edge_send, edge_recv, mom_send, mom_recv,
+    rim_send, rim_recv, edge_send, edge_recv, mom_send, mom_recv, in_sem, out_sem,
 ):
     det = lax.axis_index("det")
     tm = lax.axis_index("tm")
     me = det * NTM + tm
 
+    loads = [
+        pltpu.make_async_copy(src, dst, in_sem.at[i])
+        for i, (src, dst) in enumerate((
+            (samples_in, samples), (pointing_in, pointing), (angles_in, angles), (counts_in, counts),
+            (sky_in, sky), (prec, pp.at[:, 8:72, :]), (first_in, first), (twist_in, twist),
+            (last_in, last), (onoise_in, onoise), (oprior_in, oprior),
+        ))
+    ]
+    for load in loads:
+        load.start()
+
     ty, tz, tc = tm // 8, (tm // 2) % 4, tm % 2
-
-    def hop(d):
-        return jnp.where(d == 0, 2, jnp.where(d == 1, 1, jnp.where(d == 2, 3, 0)))
-
-    def other_tm(e):
-        y = (ty + hop(e // 8)) % 4
-        z = (tz + hop((e // 2) % 4)) % 4
-        return y * 8 + z * 2 + (tc + 1 - e % 2) % 2
+    at_z = [(tz + o) % 4 * 2 for o in range(4)]
+    at_c = [tc, 1 - tc]
+    at_det = [(det + o) % NDET for o in range(NDET)]
+
+    def to_tm(act):
+        def row(y, own):
+            for z in (2, 1, 3, 0):
+                for c in (1, 0):
+                    if not (own and z == 0 and c == 0):
+                        act(y * 8 + at_z[z] + at_c[c])
+
+        @pl.loop(0, 3)
+        def _(d):
+            row((ty + jnp.where(d == 0, 2, jnp.where(d == 1, 1, 3))) % 4, False)
+
+        row(ty, True)
 
     def to_all(act):
-        @pl.loop(0, NTM - 1)
-        def _(e):
-            to = other_tm(e)
-            for x in (2, 1, 3, 0):
-                act(((det + x) % NDET, to))
-
+        to_tm(lambda to: [act((at_det[x], to)) for x in (2, 1, 3, 0)])
         for x in (2, 1, 3):
-            act(((det + x) % NDET, tm))
+            act((at_det[x], tm))
 
     barrier = pltpu.get_barrier_semaphore()
     to_all(lambda to: pl.semaphore_signal(barrier, inc=1, device_id=to, device_id_type=MESH))
+
+    for load in loads[:4]:
+        load.wait()
 
     row_i = lax.broadcasted_iota(jnp.int32, (128, 128), 0)
     col_i = lax.broadcasted_iota(jnp.int32, (128, 128), 1)
@@ -126,6 +145,8 @@
     sbuf[pl.ds(6, 128, stride=8), :] = count_full
     sbuf[pl.ds(7, 128, stride=8), :] = count_full
 
+    loads[4].wait()
+
     for c in range(3):
         blocks = []
         for cyc in range(2):
@@ -136,7 +157,6 @@
         table[pl.ds(c * 64, 64), :] = upper
         table[pl.ds(192 + c * 64, 64), :] = (full - upper.astype(F32)).astype(BF16)
 
-    pp[:, 8:72, :] = prec[...]
     bw[:, 0:8, :] = jnp.zeros((7, 8, 128), F32)
     bw[:, 72:80, :] = jnp.zeros((7, 8, 128), F32)
 
@@ -183,8 +203,8 @@
     def edge_copies(rows, side, padded, to):
         pairs = (
             (prec.at[:, rows, :], pp.at[:, padded, :]),
-            (onoise.at[:, rows, :], edge.at[side, 0:6]),
-            (oprior.at[:, rows, :], edge.at[side, 6:12]),
+            (onoise_in.at[:, rows, :], edge.at[side, 0:6]),
+            (oprior_in.at[:, rows, :], edge.at[side, 6:12]),
         )
         return [
             pltpu.make_async_remote_copy(
@@ -328,6 +348,8 @@
 
     field = acc[:192] + acc[192:]
 
+    for load in loads[6:9]:
+        load.wait()
     z_parts = []
     for cyc in range(2):
         y = dot3(split_parts(field[:, cyc * 128 : cyc * 128 + 128]), (first[0], first[1]))
@@ -358,26 +380,36 @@
 
     @pl.when(low_end)
     def _():
-        @pl.loop(0, NTM)
-        def _(e):
-            send_spectrum(det - 1, other_tm(e), 34 + tm, rim_send, rim_recv.at[1])
+        send = lambda to: send_spectrum(det - 1, to, 34 + tm, rim_send, rim_recv.at[1])
+        to_tm(send)
+        send(tm)
 
     @pl.when(high_end)
     def _():
-        @pl.loop(0, NTM)
-        def _(e):
-            send_spectrum(det + 1, other_tm(e), tm - (NTM - 2), rim_send, rim_recv.at[0])
-
-    @pl.loop(0, NTM - 1)
-    def _(e):
-        send_spectrum(det, other_tm(e), 2 + tm, spec_send, spec_recv)
+        send = lambda to: send_spectrum(det + 1, to, tm - (NTM - 2), rim_send, rim_recv.at[0])
+        to_tm(send)
+        send(tm)
+
+    to_tm(lambda to: send_spectrum(det, to, 2 + tm, spec_send, spec_recv))
 
     spec_r[pl.ds((2 + tm) * 16, 16), :] = spec_s[pl.ds(tm * 16, 16), :]
     for c in range(3):
         for cyc in range(2):
-            part = field[c * 64 : c * 64 + 64, cyc * 128 : cyc * 128 + 128]
-            part = jnp.concatenate([part[:, :64], part[:, 64:]], axis=0)
-            map_out[c, pl.ds(cyc, 64, stride=2), :] = part.T
+            for part in range(2):
+                rows = pl.ds(part * 192 + c * 64, 64)
+                block = acc[rows, cyc * 128 : cyc * 128 + 128]
+                block = jnp.concatenate([block[:, :64], block[:, 64:]], axis=0)
+                map_s[part, c, pl.ds(cyc, 64, stride=2), :] = block.T
+    stores = [
+        pltpu.make_async_copy(map_s.at[0], map_upper_out, out_sem.at[0]),
+        pltpu.make_async_copy(map_s.at[1], map_lower_out, out_sem.at[1]),
+        pltpu.make_async_copy(sol_s, sol_out, out_sem.at[2]),
+    ]
+    stores[0].start()
+    stores[1].start()
+    loads[5].wait()
+    loads[9].wait()
+    loads[10].wait()
 
     @pl.when(det > 0)
     def _():
@@ -487,7 +519,9 @@
             direction = [r + beta * d for r, d in zip(resid, direction + [zero])]
             norm_now = norm_next
     for j in range(6):
-        sol_out[j] = answer[0] * bw[j, 8:72, :] + answer[1] * v1_s[j] + answer[2] * v2_s[j]
+        sol_s[j] = answer[0] * bw[j, 8:72, :] + answer[1] * v1_s[j] + answer[2] * v2_s[j]
+
+    stores[2].start()
 
     span = sbuf.at[pl.ds(0, (NDEV - 1) * 8)]
     pltpu.make_async_copy(span, span, send_sem).wait()
@@ -512,6 +546,8 @@
     def _():
         for copy in go_up:
             copy.wait_send()
+    for store in stores:
+        store.wait()
 
 
 def per_device(
@@ -520,17 +556,31 @@
     sky = sky_map.reshape(3, 2, 64, 128).transpose(0, 2, 1, 3).reshape(3, 128, 128)
     vmem = pl.BlockSpec(memory_space=pltpu.VMEM)
     dma = pltpu.SemaphoreType.DMA
-    gain, binned, solved = pl.pallas_call(
+    anywhere = pl.BlockSpec(memory_space=pl.ANY)
+    gain, upper, lower, solved = pl.pallas_call(
         kernel,
         name="gibbs_step",
         out_shape=(
             jax.ShapeDtypeStruct((1, 1), F32),
             jax.ShapeDtypeStruct((3, 128, 128), F32),
+            jax.ShapeDtypeStruct((3, 128, 128), F32),
             jax.ShapeDtypeStruct((6, 64, 128), F32),
         ),
-        in_specs=[vmem] * 11,
-        out_specs=(vmem, vmem, vmem),
+        in_specs=[anywhere] * 11,
+        out_specs=(vmem, anywhere, anywhere, anywhere),
         scratch_shapes=[
+            pltpu.VMEM((128, 256), F32),
+            pltpu.VMEM((128, 256), jnp.int32),
+            pltpu.VMEM((128, 256), F32),
+            pltpu.VMEM((1, 128), jnp.int32),
+            pltpu.VMEM((3, 128, 128), F32),
+            pltpu.VMEM((6, 64, 128), F32),
+            pltpu.VMEM((6, 64, 128), F32),
+            pltpu.VMEM((2, 128, 256), BF16),
+            pltpu.VMEM((2, 64, 128), F32),
+            pltpu.VMEM((2, 64, 128), BF16),
+            pltpu.VMEM((2, 3, 128, 128), F32),
+            pltpu.VMEM((6, 64, 128), F32),
             pltpu.VMEM((1024, 128), F32),
             pltpu.VMEM((1024, 128), F32),
             pltpu.VMEM((384, 256), BF16),
@@ -554,6 +604,7 @@
             pltpu.VMEM((NDEV, 1, 128), F32),
             dma, dma((NGROUP,)), dma, dma, dma, dma,
             dma, dma((2,)), dma((2, 3)), dma((2, 3)), dma, dma,
+            dma((11,)), dma((3,)),
         ],
         compiler_params=pltpu.CompilerParams(collective_id=0, has_side_effects=True),
     )(
@@ -567,7 +618,7 @@
         omega_prior,
         *(jnp.asarray(t) for t in tables()),
     )
-    binned = binned.reshape(3, 64, 2, 128).transpose(0, 2, 1, 3).reshape(3, 2, 8192)
+    binned = (upper + lower).reshape(3, 64, 2, 128).transpose(0, 2, 1, 3).reshape(3, 2, 8192)
     return (gain, binned, solved)
 
 

time: 64.3 us -> 62.6 us (0.974)
  Pallas kernels: 59.3 us -> 57.5 us
  other arithmetic: 0 us -> 1.76 us
  local copies, waits for them, and re-layouts: 2.34 us -> 0.68 us
    pallas_call x1, Pallas kernels: 59.3 us -> 57.5 us  [per_device(): pl.pallas_call(kernel, name='gibbs_step', out_shape=(jax.ShapeDtypeStruct...]
    add x0 -> x1, other arithmetic: none -> 1.76 us  [per_device(): upper + lower]
    unnamed x4 -> x3, local copies, waits for them, and re-layouts: 2.34 us -> 0.68 us
where the time goes in v3:
time: 62.6 us; the launch traced here: 62.4 us
  Pallas kernels  57.5 us (92%)
  between operations  2.47 us (4%)
  other arithmetic  1.76 us (3%)
  local copies, waits for them, and re-layouts  0.68 us (1%)
    pallas_call x1, Pallas kernels, per_device(): pl.pallas_call(kernel, name='gibbs_step', out_shape=(jax.ShapeDtypeStruct...  57.5 us
    add x1, other arithmetic, per_device(): upper + lower  1.76 us

profile of v3, /device:TPU:1, one launch (start us, length us, event | category | flops | bytes accessed | tf_op | source)
XLA Modules:
  0.0 62.4 jit_solution(16792005309051291605)
XLA Ops:
  0.6 57.5 %gibbs_step.1 = (f32[1,1]{1,0:T(1,128)}, f32[3,128,128]{2,1,0:T(8,128)}, f32[3,128,128]{2,1,0:T(8,128)}, f32[6,64,128]{2,1,0:T(8,128)}) custom-call(f32[128,256]{1,0:T(8,128)} %bitcast.16, s32[128,256]{1,0:T(8,128)} %bitcast.17, f32[128,256]{1,0:T(8,128)} %bitcast.18, s32[1,128]{1,0:T(1,128)} %bitcast.19, f32[3,128,128]{2,1,0:T(8,128)} %bitcast.14, ...), custom_call_target="tpu_custom_call" | custom-call | tf_op jit(solution)/shard_map/gibbs_step/pallas_call | solution.py:560
  58.2 0.0 copy-start
  58.2 1.8 %add.3 = f32[3,128,128]{2,1,0:T(8,128)} add(f32[3,128,128]{2,1,0:T(8,128)} %get-tuple-element.8, f32[3,128,128]{2,1,0:T(8,128)} %get-tuple-element.9) | non-fusion elementwise | flops 49152 | bytes 589824 | tf_op jit(solution)/shard_map/add | solution.py:621
  60.6 0.0 copy-done
  60.6 0.7 %copy.19 = f32[6,64,128]{2,1,0:T(8,128)} copy(f32[6,64,128]{2,1,0:T(8,128)S(1)} %copy-done) | data formatting | bytes 393216
Async XLA Ops:
  58.2 2.5 %copy-start = (f32[6,64,128]{2,1,0:T(8,128)S(1)}, f32[6,64,128]{2,1,0:T(8,128)}, u32[]{:S(2)}) copy-start(f32[6,64,128]{2,1,0:T(8,128)} %get-tuple-element.16) | copy-start | bytes 589828

commit v4 on v3

--- a/solution.py
+++ b/solution.py
@@ -16,10 +16,21 @@
 NDEV = NDET * NTM
 GROUP = 16
 NGROUP = NDEV // GROUP
-UNROLL = 16
+UNROLL = 32
 SHIFT = 4.0
 SCALE = 4.0
 STEP_MAX = 20.0
+
+
+def near_first():
+    ring = (0, 1, 2, 1)
+    return sorted(
+        ((x, y, z, c) for x in range(4) for y in range(4) for z in range(4) for c in range(2)),
+        key=lambda o: 4 * (ring[o[0]] + ring[o[1]] + ring[o[2]]) + o[3],
+    )
+
+
+NEAR = near_first()
 
 
 def tables():
@@ -40,7 +51,9 @@
         upper = x.astype(np.float32).astype(jnp.bfloat16)
         return np.stack([upper, (x - upper.astype(np.float64)).astype(jnp.bfloat16)])
 
-    return [split(first), twist.astype(np.float32), split(last)]
+    codes = np.asarray([o[0] + 4 * o[1] + 16 * o[2] + 64 * o[3] for o in NEAR], np.int32)
+    codes = np.ascontiguousarray(np.broadcast_to(codes[:, None], (NDEV, 128)))
+    return [split(first), twist.astype(np.float32), split(last), codes]
 
 
 def split_parts(x):
@@ -80,9 +93,9 @@
 
 def kernel(
     samples_in, pointing_in, angles_in, counts_in, sky_in, prec, onoise_in, oprior_in,
-    first_in, twist_in, last_in,
-    gain_out, map_upper_out, map_lower_out, sol_out,
-    samples, pointing, angles, counts, sky, onoise, oprior, first, twist, last, map_s, sol_s,
+    first_in, twist_in, last_in, codes_in,
+    small_out, map_out, basis_out,
+    samples, pointing, angles, counts, sky, onoise, oprior, first, twist, last, codes, map_s, match_s,
     sbuf, rbuf, table, hi_s, lo_s, cos_s, sin_s, look, sums_s, wsplit, acc,
     stat_r, spec_s, spec_r, pp, root_s, edge, bw, v1_s, v2_s, mom_r,
     send_sem, recv_sem, stat_send, stat_recv, spec_send, spec_recv,
@@ -97,7 +110,7 @@
         for i, (src, dst) in enumerate((
             (samples_in, samples), (pointing_in, pointing), (angles_in, angles), (counts_in, counts),
             (sky_in, sky), (prec, pp.at[:, 8:72, :]), (first_in, first), (twist_in, twist),
-            (last_in, last), (onoise_in, onoise), (oprior_in, oprior),
+            (last_in, last), (onoise_in, onoise), (oprior_in, oprior), (codes_in, codes),
         ))
     ]
     for load in loads:
@@ -106,6 +119,7 @@
     ty, tz, tc = tm // 8, (tm // 2) % 4, tm % 2
     at_z = [(tz + o) % 4 * 2 for o in range(4)]
     at_c = [tc, 1 - tc]
+    at_y = [(ty + o) % 4 * 8 for o in range(4)]
     at_det = [(det + o) % NDET for o in range(NDET)]
 
     def to_tm(act):
@@ -164,38 +178,32 @@
     def _():
         pp[:, 0:8, :] = jnp.zeros((3, 8, 128), F32)
         edge[0] = jnp.zeros((12, 8, 128), F32)
-        spec_r[0:32, :] = jnp.zeros((32, 128), F32)
+        spec_r[0:24, :] = jnp.zeros((24, 128), F32)
 
     @pl.when(det == NDET - 1)
     def _():
         pp[:, 72:80, :] = jnp.zeros((3, 8, 128), F32)
         edge[1] = jnp.zeros((12, 8, 128), F32)
-        spec_r[34 * 16 : 36 * 16, :] = jnp.zeros((32, 128), F32)
-
+        spec_r[67 * 8 : 70 * 8, :] = jnp.zeros((24, 128), F32)
+
+    loads[11].wait()
+    code = codes[...]
+    source = ((code & 3) + det) % 4 * 32 + (((code >> 2) & 3) + ty) % 4 * 8
+    source = source + (((code >> 4) & 3) + tz) % 4 * 2 + ((code >> 6) + tc) % 2
+    match_s[...] = jnp.where(source == col_i, 1.0, 0.0)
     acc[...] = jnp.zeros_like(acc)
     pl.semaphore_wait(barrier, NDEV - 1)
 
-    my_group = me // GROUP
-    my_slot = me % GROUP
-    my_tile = rbuf.at[pl.ds(me * 8, 8)]
-
-    def send_samples(group, v):
-        slot = (my_slot + v) % GROUP
+    for s, (x, y, z, c) in enumerate(NEAR):
+        if s == 0:
+            continue
+        where = at_det[-x % 4]
+        to = at_y[-y % 4] + at_z[-z % 4] + at_c[c]
         pltpu.make_async_remote_copy(
-            sbuf.at[pl.ds((group * GROUP + slot) * 8, 8)], my_tile, send_sem, recv_sem.at[my_group],
-            device_id=(group // 2, (group % 2) * GROUP + slot), device_id_type=MESH,
+            sbuf.at[pl.ds((where * NTM + to) * 8, 8)], rbuf.at[s * 8 : s * 8 + 8],
+            send_sem, recv_sem.at[s // GROUP], device_id=(where, to), device_id_type=MESH,
         ).start()
-
-    for v in range(1, GROUP):
-        send_samples(my_group, v)
-
-    @pl.loop(1, NGROUP)
-    def _(t):
-        group = (my_group + NGROUP - t) % NGROUP
-        for v in range(GROUP):
-            send_samples(group, v)
-
-    rbuf[pl.ds(me * 8, 8), :] = sbuf[pl.ds(me * 8, 8), :]
+    rbuf[0:8, :] = sbuf[pl.ds(me * 8, 8), :]
 
     down = ((det + 1) % NDET, tm)
     up = ((det + NDET - 1) % NDET, tm)
@@ -242,32 +250,27 @@
             upper = (pixel >> 13) * 128 + ((pixel >> 6) & 1) * 64 + ((pixel >> 7) & 63)
             hi_s[half, here, :] = upper.astype(F32)
             lo_s[half, here, :] = (pixel & 63).astype(F32)
-            sine, cosine = sine_cosine(2.0 * row(2 + half))
-            sin_s[half, here, :] = sine
-            cos_s[half, here, :] = cosine
-        for first_s in range(0, GROUP, UNROLL):
-            for u in range(UNROLL):
-                s = base + first_s + u
-                hots = [one_hot(hi_s[half, pl.ds(s, 1), :], 256) for half in range(2)]
-                got = jnp.dot(table[...], jnp.concatenate(hots, axis=1), preferred_element_type=F32)
-                got = got[:192] + got[192:]
-                for half in range(2):
-                    low = lo_s[half, pl.ds(s, 1), :]
-                    same = col_index == low
-                    for c in range(3):
-                        part = got[c * 64 : c * 64 + 64, half * 128 : half * 128 + 128]
-                        look[c, half, pl.ds(s, 1), :] = jnp.sum(
-                            jnp.where(same, part, 0.0), axis=0, keepdims=True
-                        )
+        for u in range(GROUP):
+            s = base + u
+            hots = [one_hot(hi_s[half, pl.ds(s, 1), :], 256) for half in range(2)]
+            got = jnp.dot(table[...], jnp.concatenate(hots, axis=1), preferred_element_type=F32)
+            got = got[:192] + got[192:]
+            for half in range(2):
+                low = lo_s[half, pl.ds(s, 1), :]
+                same = col_index == low
+                for c in range(3):
+                    part = got[c * 64 : c * 64 + 64, half * 128 : half * 128 + 128]
+                    look[c, half, pl.ds(s, 1), :] = jnp.sum(
+                        jnp.where(same, part, 0.0), axis=0, keepdims=True
+                    )
         count = row(6)
         cross = jnp.zeros((GROUP, 128), F32)
         square = jnp.zeros((GROUP, 128), F32)
         for half in range(2):
-            signal = (
-                look[0, half, here, :]
-                + look[1, half, here, :] * cos_s[half, here, :]
-                + look[2, half, here, :] * sin_s[half, here, :]
-            )
+            sine, cosine = sine_cosine(2.0 * row(2 + half))
+            sin_s[half, here, :] = sine
+            cos_s[half, here, :] = cosine
+            signal = look[0, half, here, :] + look[1, half, here, :] * cosine + look[2, half, here, :] * sine
             look[0, half, here, :] = signal
             masked = jnp.where(slot_index + 128.0 * half < count, signal, 0.0)
             cross = cross + masked * row(half)
@@ -276,23 +279,26 @@
         sums_s[1, here, :] = square
 
     @pl.loop(0, NGROUP)
-    def _(t):
-        group = (my_group + t) % NGROUP
-
-        @pl.when(t == 0)
+    def _(group):
+        @pl.when(group == 0)
         def _():
             span = rbuf.at[pl.ds(0, (GROUP - 1) * 8)]
-            pltpu.make_async_copy(span, span, recv_sem.at[my_group]).wait()
-
-        @pl.when(t > 0)
+            pltpu.make_async_copy(span, span, recv_sem.at[0]).wait()
+
+        @pl.when(group > 0)
         def _():
             span = rbuf.at[pl.ds(0, GROUP * 8)]
             pltpu.make_async_copy(span, span, recv_sem.at[group]).wait()
 
         gather_group(group)
 
-    cross = jnp.sum(sums_s[0].T, axis=0, keepdims=True)
-    square = jnp.sum(sums_s[1].T, axis=0, keepdims=True)
+    match = match_s[...] > 0.5
+    cross, square = (
+        jnp.sum(
+            jnp.where(match, jnp.sum(sums_s[k], axis=1, keepdims=True), 0.0), axis=0, keepdims=True
+        )
+        for k in range(2)
+    )
     mine = stat_r.at[me]
     mine[...] = jnp.concatenate([cross, square], axis=0)
     to_all(
@@ -307,8 +313,9 @@
     total = jnp.sum(stat_r[...], axis=0)
     gains = total[0:1] / (total[1:2] + 1e-06)
     lane = lax.broadcasted_iota(jnp.int32, (1, 128), 1)
-    gain_out[...] = jnp.sum(jnp.where(lane == me, gains, 0.0), axis=1, keepdims=True)
-    gain_full = jnp.broadcast_to(gains, (128, 128)).T
+    own_gain = jnp.sum(jnp.where(lane == me, gains, 0.0), axis=1, keepdims=True)
+    gain_col = jnp.sum(jnp.where(match, gains, 0.0), axis=1, keepdims=True)
+    gain_full = jnp.broadcast_to(gain_col, (128, 128))
 
     hits = [jnp.zeros((1, 128), F32) for _ in range(2)]
     for half in range(2):
@@ -363,50 +370,51 @@
     for cyc in range(2):
         for c in range(3):
             block = x[:, (cyc * 3 + c) * 128 : (cyc * 3 + c) * 128 + 128]
-            spec_s[pl.ds(4 * c + cyc, 32, stride=16), :] = block[:32]
-            spec_s[pl.ds(4 * c + 2 + cyc, 32, stride=16), :] = block[32:]
+            spec_s[pl.ds(cyc * 8 + 2 * c, 32, stride=16), :] = block[:32]
+            spec_s[pl.ds(cyc * 8 + 2 * c + 1, 32, stride=16), :] = block[32:]
         weight = jnp.sum(hits[cyc], axis=1, keepdims=True) * (1.0 / 8192)
-        spec_s[pl.ds(12 + cyc, 32, stride=16), :] = jnp.broadcast_to(weight, (32, 128))
-        spec_s[pl.ds(14 + cyc, 32, stride=16), :] = jnp.broadcast_to(weight, (32, 128))
-
-    def send_spectrum(where, to, slot, send, recv):
+        for r in (6, 7):
+            spec_s[pl.ds(cyc * 8 + r, 32, stride=16), :] = jnp.broadcast_to(weight, (32, 128))
+
+    def send_spectrum(where, to, skip, tiles, slot, send, recv):
         pltpu.make_async_remote_copy(
-            spec_s.at[pl.ds(to * 16, 16)], spec_r.at[pl.ds(slot * 16, 16)],
+            spec_s.at[pl.ds(to * 16 + skip * 8, tiles * 8)], spec_r.at[pl.ds(slot * 8, tiles * 8)],
             send, recv, device_id=(where, to), device_id_type=MESH,
         ).start()
 
-    low_end = jnp.logical_and(tm < 2, det > 0)
-    high_end = jnp.logical_and(tm >= NTM - 2, det < NDET - 1)
-
-    @pl.when(low_end)
-    def _():
-        send = lambda to: send_spectrum(det - 1, to, 34 + tm, rim_send, rim_recv.at[1])
+    def send_rim(where, skip, tiles, slot, recv):
+        send = lambda to: send_spectrum(where, to, skip, tiles, slot, rim_send, recv)
         to_tm(send)
         send(tm)
 
-    @pl.when(high_end)
-    def _():
-        send = lambda to: send_spectrum(det + 1, to, tm - (NTM - 2), rim_send, rim_recv.at[0])
-        to_tm(send)
-        send(tm)
-
-    to_tm(lambda to: send_spectrum(det, to, 2 + tm, spec_send, spec_recv))
-
-    spec_r[pl.ds((2 + tm) * 16, 16), :] = spec_s[pl.ds(tm * 16, 16), :]
+    rims = []
+    for at, bound, step, skip, tiles, slot, side in (
+        (0, det > 0, -1, 0, 2, 67, 1),
+        (1, det > 0, -1, 0, 1, 69, 1),
+        (NTM - 2, det < NDET - 1, 1, 1, 1, 0, 0),
+        (NTM - 1, det < NDET - 1, 1, 0, 2, 1, 0),
+    ):
+        here = jnp.logical_and(tm == at, bound)
+        rims.append((here, tiles))
+
+        @pl.when(here)
+        def _():
+            send_rim(det + step, skip, tiles, slot, rim_recv.at[side])
+
+    to_tm(lambda to: send_spectrum(det, to, 0, 2, 3 + 2 * tm, spec_send, spec_recv))
+    spec_r[pl.ds((3 + 2 * tm) * 8, 16), :] = spec_s[pl.ds(tm * 16, 16), :]
     for c in range(3):
         for cyc in range(2):
-            for part in range(2):
-                rows = pl.ds(part * 192 + c * 64, 64)
-                block = acc[rows, cyc * 128 : cyc * 128 + 128]
-                block = jnp.concatenate([block[:, :64], block[:, 64:]], axis=0)
-                map_s[part, c, pl.ds(cyc, 64, stride=2), :] = block.T
+            block = field[c * 64 : c * 64 + 64, cyc * 128 : cyc * 128 + 128]
+            block = jnp.concatenate([block[:, :64], block[:, 64:]], axis=0)
+            map_s[c, pl.ds(cyc, 64, stride=2), :] = block.T
     stores = [
-        pltpu.make_async_copy(map_s.at[0], map_upper_out, out_sem.at[0]),
-        pltpu.make_async_copy(map_s.at[1], map_lower_out, out_sem.at[1]),
-        pltpu.make_async_copy(sol_s, sol_out, out_sem.at[2]),
+        pltpu.make_async_copy(map_s, map_out, out_sem.at[0]),
+        pltpu.make_async_copy(bw.at[0:6, 8:72, :], basis_out.at[0], out_sem.at[1]),
+        pltpu.make_async_copy(v1_s, basis_out.at[1], out_sem.at[2]),
+        pltpu.make_async_copy(v2_s, basis_out.at[2], out_sem.at[3]),
     ]
     stores[0].start()
-    stores[1].start()
     loads[5].wait()
     loads[9].wait()
     loads[10].wait()
@@ -426,20 +434,19 @@
 
     @pl.when(det > 0)
     def _():
-        span = spec_r.at[pl.ds(0, 32)]
+        span = spec_r.at[pl.ds(0, 24)]
         pltpu.make_async_copy(span, span, rim_recv.at[0]).wait()
 
     @pl.when(det < NDET - 1)
     def _():
-        span = spec_r.at[pl.ds(0, 32)]
+        span = spec_r.at[pl.ds(0, 24)]
         pltpu.make_async_copy(span, span, rim_recv.at[1]).wait()
 
     span = spec_r.at[pl.ds(0, (NTM - 1) * 16)]
     pltpu.make_async_copy(span, span, spec_recv).wait()
 
-    for cyc in range(2):
-        for j in range(7):
-            bw[j, pl.ds(4 + cyc, 36, stride=2), :] = spec_r[pl.ds(2 * j + cyc, 36, stride=16), :]
+    for j in range(7):
+        bw[j, 5:75, :] = spec_r[pl.ds(j, 70, stride=8), :]
     noise_root = jnp.sqrt(bw[6])
     for j in range(6):
         noise = jnp.concatenate([edge[0, j], onoise[j], edge[1, j]], axis=0)
@@ -480,6 +487,8 @@
             own_row, own_row, mom_send, mom_recv, device_id=to, device_id_type=MESH
         ).start()
     )
+    for store in stores[1:]:
+        store.start()
     rest = mom_r.at[pl.ds(0, NDEV - 1)]
     pltpu.make_async_copy(rest, rest, mom_recv).wait()
     sums = jnp.sum(mom_r[...], axis=0)
@@ -518,10 +527,8 @@
             beta = norm_next / norm_now
             direction = [r + beta * d for r, d in zip(resid, direction + [zero])]
             norm_now = norm_next
-    for j in range(6):
-        sol_s[j] = answer[0] * bw[j, 8:72, :] + answer[1] * v1_s[j] + answer[2] * v2_s[j]
-
-    stores[2].start()
+    for i, value in enumerate(answer + [own_gain]):
+        small_out[i : i + 1, :] = jnp.broadcast_to(value, (1, 128))
 
     span = sbuf.at[pl.ds(0, (NDEV - 1) * 8)]
     pltpu.make_async_copy(span, span, send_sem).wait()
@@ -532,10 +539,11 @@
     rest = mom_r.at[pl.ds(0, NDEV - 1)]
     pltpu.make_async_copy(rest, rest, mom_send).wait()
 
-    @pl.when(jnp.logical_or(low_end, high_end))
-    def _():
-        span = spec_s.at[pl.ds(0, NTM * 16)]
-        pltpu.make_async_copy(span, span, rim_send).wait()
+    for here, tiles in rims:
+        @pl.when(here)
+        def _():
+            span = spec_s.at[pl.ds(0, NTM * tiles * 8)]
+            pltpu.make_async_copy(span, span, rim_send).wait()
 
     @pl.when(det < NDET - 1)
     def _():
@@ -546,6 +554,28 @@
     def _():
         for copy in go_up:
             copy.wait_send()
+    for store in stores:
+        store.wait()
+
+
+def finish(small, map_in, basis_in, gain_out, map_out, sol_out, map_s, basis, sol_s, in_sem, out_sem):
+    loads = [pltpu.make_async_copy(basis_in.at[i], basis.at[i], in_sem.at[i]) for i in range(3)]
+    loads.append(pltpu.make_async_copy(map_in, map_s, in_sem.at[3]))
+    for load in loads:
+        load.start()
+    gain_out[...] = small[3:4, 0:1]
+    for load in loads[:3]:
+        load.wait()
+    parts = [jnp.broadcast_to(small[i : i + 1, :], (64, 128)) for i in range(3)]
+    for j in range(6):
+        sol_s[j] = parts[0] * basis[0, j] + parts[1] * basis[1, j] + parts[2] * basis[2, j]
+    stores = [
+        pltpu.make_async_copy(sol_s, sol_out, out_sem.at[0]),
+        pltpu.make_async_copy(map_s, map_out, out_sem.at[1]),
+    ]
+    stores[0].start()
+    loads[3].wait()
+    stores[1].start()
     for store in stores:
         store.wait()
 
@@ -557,17 +587,16 @@
     vmem = pl.BlockSpec(memory_space=pltpu.VMEM)
     dma = pltpu.SemaphoreType.DMA
     anywhere = pl.BlockSpec(memory_space=pl.ANY)
-    gain, upper, lower, solved = pl.pallas_call(
+    small, binned, basis = pl.pallas_call(
         kernel,
         name="gibbs_step",
         out_shape=(
-            jax.ShapeDtypeStruct((1, 1), F32),
+            jax.ShapeDtypeStruct((8, 128), F32),
             jax.ShapeDtypeStruct((3, 128, 128), F32),
-            jax.ShapeDtypeStruct((3, 128, 128), F32),
-            jax.ShapeDtypeStruct((6, 64, 128), F32),
+            jax.ShapeDtypeStruct((3, 6, 64, 128), F32),
         ),
-        in_specs=[anywhere] * 11,
-        out_specs=(vmem, anywhere, anywhere, anywhere),
+        in_specs=[anywhere] * 12,
+        out_specs=(vmem, anywhere, anywhere),
         scratch_shapes=[
             pltpu.VMEM((128, 256), F32),
             pltpu.VMEM((128, 256), jnp.int32),
@@ -579,8 +608,9 @@
             pltpu.VMEM((2, 128, 256), BF16),
             pltpu.VMEM((2, 64, 128), F32),
             pltpu.VMEM((2, 64, 128), BF16),
-            pltpu.VMEM((2, 3, 128, 128), F32),
-            pltpu.VMEM((6, 64, 128), F32),
+            pltpu.VMEM((NDEV, 128), jnp.int32),
+            pltpu.VMEM((3, 128, 128), F32),
+            pltpu.VMEM((NDEV, 128), F32),
             pltpu.VMEM((1024, 128), F32),
             pltpu.VMEM((1024, 128), F32),
             pltpu.VMEM((384, 256), BF16),
@@ -594,7 +624,7 @@
             pltpu.VMEM((384, 256), F32),
             pltpu.VMEM((NDEV, 2, 128), F32),
             pltpu.VMEM((NTM * 16, 128), F32),
-            pltpu.VMEM(((NTM + 4) * 16, 128), F32),
+            pltpu.VMEM((70 * 8, 128), F32),
             pltpu.VMEM((3, 80, 128), F32),
             pltpu.VMEM((3, 80, 128), F32),
             pltpu.VMEM((2, 12, 8, 128), F32),
@@ -604,7 +634,7 @@
             pltpu.VMEM((NDEV, 1, 128), F32),
             dma, dma((NGROUP,)), dma, dma, dma, dma,
             dma, dma((2,)), dma((2, 3)), dma((2, 3)), dma, dma,
-            dma((11,)), dma((3,)),
+            dma((12,)), dma((4,)),
         ],
         compiler_params=pltpu.CompilerParams(collective_id=0, has_side_effects=True),
     )(
@@ -618,7 +648,24 @@
         omega_prior,
         *(jnp.asarray(t) for t in tables()),
     )
-    binned = (upper + lower).reshape(3, 64, 2, 128).transpose(0, 2, 1, 3).reshape(3, 2, 8192)
+    gain, binned, solved = pl.pallas_call(
+        finish,
+        name="finish",
+        out_shape=(
+            jax.ShapeDtypeStruct((1, 1), F32),
+            jax.ShapeDtypeStruct((3, 128, 128), F32),
+            jax.ShapeDtypeStruct((6, 64, 128), F32),
+        ),
+        in_specs=[vmem, anywhere, anywhere],
+        out_specs=(vmem, anywhere, anywhere),
+        scratch_shapes=[
+            pltpu.VMEM((3, 128, 128), F32),
+            pltpu.VMEM((3, 6, 64, 128), F32),
+            pltpu.VMEM((6, 64, 128), F32),
+            dma((4,)), dma((2,)),
+        ],
+    )(small, binned, basis)
+    binned = binned.reshape(3, 64, 2, 128).transpose(0, 2, 1, 3).reshape(3, 2, 8192)
     return (gain, binned, solved)
 
 

time: 62.6 us -> 56.1 us (0.90)
  Pallas kernels: 57.5 us -> 55.3 us
  between operations: 2.47 us -> 0.64 us
  other arithmetic: 1.76 us -> 0 us
  local copies, waits for them, and re-layouts: 0.68 us -> 0 us
    pallas_call x1, Pallas kernels: 57.5 us -> 52.1 us  [per_device(): pl.pallas_call(kernel, name='gibbs_step', out_shape=(jax.ShapeDtypeStruct...]
    pallas_call x0 -> x1, Pallas kernels: none -> 3.13 us  [per_device(): pl.pallas_call(finish, name='finish', out_shape=(jax.ShapeDtypeStruct((1,...]
    add x1 -> x0, other arithmetic: 1.76 us -> none  [per_device(): upper + lower]
    unnamed x3 -> x0, local copies, waits for them, and re-layouts: 0.68 us -> none
where the time goes in v4:
time: 56.1 us; the launch traced here: 55.9 us
  Pallas kernels  55.3 us (99%)
  between operations  0.64 us (1%)
    pallas_call x1, Pallas kernels, per_device(): pl.pallas_call(kernel, name='gibbs_step', out_shape=(jax.ShapeDtypeStruct...  52.1 us
    pallas_call x1, Pallas kernels, per_device(): pl.pallas_call(finish, name='finish', out_shape=(jax.ShapeDtypeStruct((1,...  3.13 us

profile of v4, /device:TPU:1, one launch (start us, length us, event | category | flops | bytes accessed | tf_op | source)
XLA Modules:
  0.0 55.9 jit_solution(3067983362588191343)
XLA Ops:
  0.6 52.1 %gibbs_step.1 = (f32[8,128]{1,0:T(8,128)}, f32[3,128,128]{2,1,0:T(8,128)}, f32[3,6,64,128]{3,2,1,0:T(8,128)}) custom-call(f32[128,256]{1,0:T(8,128)} %bitcast.15, s32[128,256]{1,0:T(8,128)} %bitcast.16, f32[128,256]{1,0:T(8,128)} %bitcast.17, s32[1,128]{1,0:T(1,128)} %bitcast.18, f32[3,128,128]{2,1,0:T(8,128)} %bitcast.14, f32[3,64,128]{2,1,0:T(8,128)} %prec.1, ...), custom_call_target="tpu_custom_call" | custom-call | tf_op jit(solution)/shard_map/gibbs_step/pallas_call | solution.py:590
  52.8 3.1 %finish.1 = (f32[1,1]{1,0:T(1,128)}, f32[3,128,128]{2,1,0:T(8,128)}, f32[6,64,128]{2,1,0:T(8,128)}) custom-call(f32[8,128]{1,0:T(8,128)} %get-tuple-element.9.small, f32[3,128,128]{2,1,0:T(8,128)} %get-tuple-element.10.map_in, f32[3,6,64,128]{3,2,1,0:T(8,128)} %get-tuple-element.11.basis_in), custom_call_target="tpu_custom_call" | custom-call | tf_op jit(solution)/shard_map/finish/pallas_call | solution.py:651

commit v5 on v4

--- a/solution.py
+++ b/solution.py
@@ -94,12 +94,12 @@
 def kernel(
     samples_in, pointing_in, angles_in, counts_in, sky_in, prec, onoise_in, oprior_in,
     first_in, twist_in, last_in, codes_in,
-    small_out, map_out, basis_out,
-    samples, pointing, angles, counts, sky, onoise, oprior, first, twist, last, codes, map_s, match_s,
+    small_out, map_s, sol_out,
+    samples, pointing, angles, counts, sky, onoise, oprior, first, twist, last, codes, match_s,
     sbuf, rbuf, table, hi_s, lo_s, cos_s, sin_s, look, sums_s, wsplit, acc,
     stat_r, spec_s, spec_r, pp, root_s, edge, bw, v1_s, v2_s, mom_r,
     send_sem, recv_sem, stat_send, stat_recv, spec_send, spec_recv,
-    rim_send, rim_recv, edge_send, edge_recv, mom_send, mom_recv, in_sem, out_sem,
+    rim_send, rim_recv, edge_send, edge_recv, mom_send, mom_recv, in_sem,
 ):
     det = lax.axis_index("det")
     tm = lax.axis_index("tm")
@@ -408,13 +408,6 @@
             block = field[c * 64 : c * 64 + 64, cyc * 128 : cyc * 128 + 128]
             block = jnp.concatenate([block[:, :64], block[:, 64:]], axis=0)
             map_s[c, pl.ds(cyc, 64, stride=2), :] = block.T
-    stores = [
-        pltpu.make_async_copy(map_s, map_out, out_sem.at[0]),
-        pltpu.make_async_copy(bw.at[0:6, 8:72, :], basis_out.at[0], out_sem.at[1]),
-        pltpu.make_async_copy(v1_s, basis_out.at[1], out_sem.at[2]),
-        pltpu.make_async_copy(v2_s, basis_out.at[2], out_sem.at[3]),
-    ]
-    stores[0].start()
     loads[5].wait()
     loads[9].wait()
     loads[10].wait()
@@ -487,8 +480,6 @@
             own_row, own_row, mom_send, mom_recv, device_id=to, device_id_type=MESH
         ).start()
     )
-    for store in stores[1:]:
-        store.start()
     rest = mom_r.at[pl.ds(0, NDEV - 1)]
     pltpu.make_async_copy(rest, rest, mom_recv).wait()
     sums = jnp.sum(mom_r[...], axis=0)
@@ -527,8 +518,9 @@
             beta = norm_next / norm_now
             direction = [r + beta * d for r, d in zip(resid, direction + [zero])]
             norm_now = norm_next
-    for i, value in enumerate(answer + [own_gain]):
-        small_out[i : i + 1, :] = jnp.broadcast_to(value, (1, 128))
+    small_out[...] = jnp.broadcast_to(own_gain, (8, 128))
+    for j in range(6):
+        sol_out[j] = answer[0] * bw[j, 8:72, :] + answer[1] * v1_s[j] + answer[2] * v2_s[j]
 
     span = sbuf.at[pl.ds(0, (NDEV - 1) * 8)]
     pltpu.make_async_copy(span, span, send_sem).wait()
@@ -554,28 +546,16 @@
     def _():
         for copy in go_up:
             copy.wait_send()
+
+
+def finish(small, map_in, sol_in, gain_out, map_out, sol_out, out_sem):
+    stores = [
+        pltpu.make_async_copy(sol_in, sol_out, out_sem.at[0]),
+        pltpu.make_async_copy(map_in, map_out, out_sem.at[1]),
+    ]
     for store in stores:
-        store.wait()
-
-
-def finish(small, map_in, basis_in, gain_out, map_out, sol_out, map_s, basis, sol_s, in_sem, out_sem):
-    loads = [pltpu.make_async_copy(basis_in.at[i], basis.at[i], in_sem.at[i]) for i in range(3)]
-    loads.append(pltpu.make_async_copy(map_in, map_s, in_sem.at[3]))
-    for load in loads:
-        load.start()
-    gain_out[...] = small[3:4, 0:1]
-    for load in loads[:3]:
-        load.wait()
-    parts = [jnp.broadcast_to(small[i : i + 1, :], (64, 128)) for i in range(3)]
-    for j in range(6):
-        sol_s[j] = parts[0] * basis[0, j] + parts[1] * basis[1, j] + parts[2] * basis[2, j]
-    stores = [
-        pltpu.make_async_copy(sol_s, sol_out, out_sem.at[0]),
-        pltpu.make_async_copy(map_s, map_out, out_sem.at[1]),
-    ]
-    stores[0].start()
-    loads[3].wait()
-    stores[1].start()
+        store.start()
+    gain_out[...] = small[0:1, 0:1]
     for store in stores:
         store.wait()
 
@@ -587,16 +567,16 @@
     vmem = pl.BlockSpec(memory_space=pltpu.VMEM)
     dma = pltpu.SemaphoreType.DMA
     anywhere = pl.BlockSpec(memory_space=pl.ANY)
-    small, binned, basis = pl.pallas_call(
+    small, binned, solved = pl.pallas_call(
         kernel,
         name="gibbs_step",
         out_shape=(
-            jax.ShapeDtypeStruct((8, 128), F32),
-            jax.ShapeDtypeStruct((3, 128, 128), F32),
-            jax.ShapeDtypeStruct((3, 6, 64, 128), F32),
+            pltpu.VMEM((8, 128), F32),
+            pltpu.VMEM((3, 128, 128), F32),
+            pltpu.VMEM((6, 64, 128), F32),
         ),
         in_specs=[anywhere] * 12,
-        out_specs=(vmem, anywhere, anywhere),
+        out_specs=(vmem, vmem, vmem),
         scratch_shapes=[
             pltpu.VMEM((128, 256), F32),
             pltpu.VMEM((128, 256), jnp.int32),
@@ -609,7 +589,6 @@
             pltpu.VMEM((2, 64, 128), F32),
             pltpu.VMEM((2, 64, 128), BF16),
             pltpu.VMEM((NDEV, 128), jnp.int32),
-            pltpu.VMEM((3, 128, 128), F32),
             pltpu.VMEM((NDEV, 128), F32),
             pltpu.VMEM((1024, 128), F32),
             pltpu.VMEM((1024, 128), F32),
@@ -634,7 +613,7 @@
             pltpu.VMEM((NDEV, 1, 128), F32),
             dma, dma((NGROUP,)), dma, dma, dma, dma,
             dma, dma((2,)), dma((2, 3)), dma((2, 3)), dma, dma,
-            dma((12,)), dma((4,)),
+            dma((12,)),
         ],
         compiler_params=pltpu.CompilerParams(collective_id=0, has_side_effects=True),
     )(
@@ -656,15 +635,10 @@
             jax.ShapeDtypeStruct((3, 128, 128), F32),
             jax.ShapeDtypeStruct((6, 64, 128), F32),
         ),
-        in_specs=[vmem, anywhere, anywhere],
+        in_specs=[vmem, vmem, vmem],
         out_specs=(vmem, anywhere, anywhere),
-        scratch_shapes=[
-            pltpu.VMEM((3, 128, 128), F32),
-            pltpu.VMEM((3, 6, 64, 128), F32),
-            pltpu.VMEM((6, 64, 128), F32),
-            dma((4,)), dma((2,)),
-        ],
-    )(small, binned, basis)
+        scratch_shapes=[dma((2,))],
+    )(*(pltpu.with_memory_space_constraint(x, pltpu.VMEM) for x in (small, binned, solved)))
     binned = binned.reshape(3, 64, 2, 128).transpose(0, 2, 1, 3).reshape(3, 2, 8192)
     return (gain, binned, solved)
 

time: 56.1 us -> 53.6 us (0.955)
  Pallas kernels: 55.3 us -> 52.8 us
    pallas_call x1, Pallas kernels: 3.13 us -> 1.27 us  [per_device(): pl.pallas_call(finish, name='finish', out_shape=(jax.ShapeDtypeStruct((1,...]
    pallas_call x1, Pallas kernels: 52.1 us -> 51.5 us  [per_device(): pl.pallas_call(kernel, name='gibbs_step', out_shape=(pltpu.VMEM((8, 128),...]
where the time goes in v5:
time: 53.6 us; the launch traced here: 53.4 us
  Pallas kernels  52.8 us (99%)
  between operations  0.64 us (1%)
    pallas_call x1, Pallas kernels, per_device(): pl.pallas_call(kernel, name='gibbs_step', out_shape=(pltpu.VMEM((8, 128),...  51.5 us
    pallas_call x1, Pallas kernels, per_device(): pl.pallas_call(finish, name='finish', out_shape=(jax.ShapeDtypeStruct((1,...  1.27 us

profile of v5, /device:TPU:1, one launch (start us, length us, event | category | flops | bytes accessed | tf_op | source)
XLA Modules:
  0.0 53.4 jit_solution(819356709773826317)
XLA Ops:
  0.6 51.5 %gibbs_step.1 = (f32[8,128]{1,0:T(8,128)S(1)}, f32[3,128,128]{2,1,0:T(8,128)S(1)}, f32[6,64,128]{2,1,0:T(8,128)S(1)}) custom-call(f32[128,256]{1,0:T(8,128)} %bitcast.15, s32[128,256]{1,0:T(8,128)} %bitcast.16, f32[128,256]{1,0:T(8,128)} %bitcast.17, s32[1,128]{1,0:T(1,128)} %bitcast.18, f32[3,128,128]{2,1,0:T(8,128)} %bitcast.14, f32[3,64,128]{2,1,0:T(8,128)} %prec.1, ...), custom_call_target="tpu_custom_call" | custom-call | tf_op jit(solution)/shard_map/gibbs_step/pallas_call | solution.py:570
  52.2 1.3 %finish.1 = (f32[1,1]{1,0:T(1,128)}, f32[3,128,128]{2,1,0:T(8,128)}, f32[6,64,128]{2,1,0:T(8,128)}) custom-call(f32[8,128]{1,0:T(8,128)S(1)} %get-tuple-element.9.small, f32[3,128,128]{2,1,0:T(8,128)S(1)} %get-tuple-element.10.map_in, f32[6,64,128]{2,1,0:T(8,128)S(1)} %get-tuple-element.11.sol_in), custom_call_target="tpu_custom_call" | custom-call | tf_op jit(solution)/shard_map/finish/pallas_call | solution.py:630

commit v6 on v5

--- a/solution.py
+++ b/solution.py
@@ -16,6 +16,7 @@
 NDEV = NDET * NTM
 GROUP = 16
 NGROUP = NDEV // GROUP
+LOWER = 12
 UNROLL = 32
 SHIFT = 4.0
 SCALE = 4.0
@@ -250,7 +251,21 @@
             upper = (pixel >> 13) * 128 + ((pixel >> 6) & 1) * 64 + ((pixel >> 7) & 63)
             hi_s[half, here, :] = upper.astype(F32)
             lo_s[half, here, :] = (pixel & 63).astype(F32)
-        for u in range(GROUP):
+        pixel = jnp.concatenate(
+            [rbuf[pl.ds((base + LOWER) * 8 + 4 + half, GROUP - LOWER, stride=8), :] for half in range(2)], axis=0
+        ).astype(jnp.int32)
+        in_row, at_lane = ((pixel >> 7) & 63) * 2 + (pixel >> 13), pixel & 127
+        picked = [jnp.zeros((8, 128), F32) for _ in range(3)]
+
+        def permute_rows(first_r, last_r):
+            for r in range(first_r, last_r):
+                same = in_row == r
+                for c in range(3):
+                    line = jnp.broadcast_to(sky[c, r : r + 1, :], (8, 128))
+                    taken = jnp.take_along_axis(line, at_lane, axis=1)
+                    picked[c] = jnp.where(same, taken, picked[c])
+
+        for u in range(LOWER):
             s = base + u
             hots = [one_hot(hi_s[half, pl.ds(s, 1), :], 256) for half in range(2)]
             got = jnp.dot(table[...], jnp.concatenate(hots, axis=1), preferred_element_type=F32)
@@ -263,6 +278,10 @@
                     look[c, half, pl.ds(s, 1), :] = jnp.sum(
                         jnp.where(same, part, 0.0), axis=0, keepdims=True
                     )
+            permute_rows(u * 128 // LOWER, (u + 1) * 128 // LOWER)
+        for half in range(2):
+            for c in range(3):
+                look[c, half, pl.ds(base + LOWER, GROUP - LOWER), :] = picked[c][half * 4 : half * 4 + 4]
         count = row(6)
         cross = jnp.zeros((GROUP, 128), F32)
         square = jnp.zeros((GROUP, 128), F32)
@@ -308,6 +327,18 @@
     )
     count = rbuf[pl.ds(6, 128, stride=8), :]
     slot = col_i.astype(F32)
+    hits = [jnp.zeros((1, 128), F32) for _ in range(2)]
+    for half in range(2):
+        good = slot + 128.0 * half < count
+        for first_w, value in ((0, rbuf[pl.ds(half, 128, stride=8), :]), (3, look[0, half])):
+            value = jnp.where(good, value, 0.0)
+            wsplit[first_w, half] = value
+            wsplit[first_w + 1, half] = value * cos_s[half]
+            wsplit[first_w + 2, half] = value * sin_s[half]
+        late = jnp.where(hi_s[half] >= 128.0, 1.0, 0.0)
+        valid = jnp.where(good, 1.0, 0.0)
+        hits[1] = hits[1] + jnp.sum(valid * late, axis=0, keepdims=True)
+        hits[0] = hits[0] + jnp.sum(valid * (1.0 - late), axis=0, keepdims=True)
     rest = stat_r.at[pl.ds(0, NDEV - 1)]
     pltpu.make_async_copy(rest, rest, stat_recv).wait()
     total = jnp.sum(stat_r[...], axis=0)
@@ -317,19 +348,12 @@
     gain_col = jnp.sum(jnp.where(match, gains, 0.0), axis=1, keepdims=True)
     gain_full = jnp.broadcast_to(gain_col, (128, 128))
 
-    hits = [jnp.zeros((1, 128), F32) for _ in range(2)]
     for half in range(2):
-        data = rbuf[pl.ds(half, 128, stride=8), :]
-        good = slot + 128.0 * half < count
-        residual = jnp.where(good, data - gain_full * look[0, half], 0.0)
-        for c, weight in enumerate((residual, residual * cos_s[half], residual * sin_s[half])):
+        for c in range(3):
+            weight = wsplit[c, half] - gain_full * wsplit[3 + c, half]
             upper = weight.astype(BF16).astype(F32)
             wsplit[c, half] = upper
             wsplit[3 + c, half] = weight - upper
-        late = jnp.where(hi_s[half] >= 128.0, 1.0, 0.0)
-        valid = jnp.where(good, 1.0, 0.0)
-        hits[1] = hits[1] + jnp.sum(valid * late, axis=0, keepdims=True)
-        hits[0] = hits[0] + jnp.sum(valid * (1.0 - late), axis=0, keepdims=True)
 
     low_index = lax.broadcasted_iota(jnp.int32, (64, 128), 0).astype(F32).astype(BF16).reshape(4, 16, 128)
 

time: 53.6 us -> 52.9 us (0.987)
  Pallas kernels: 52.8 us -> 52.2 us
    pallas_call x1, Pallas kernels: 51.5 us -> 50.9 us  [per_device(): pl.pallas_call(kernel, name='gibbs_step', out_shape=(pltpu.VMEM((8, 128),...]
where the time goes in v6:
time: 52.9 us; the launch traced here: 52.8 us
  Pallas kernels  52.2 us (99%)
  between operations  0.64 us (1%)
    pallas_call x1, Pallas kernels, per_device(): pl.pallas_call(kernel, name='gibbs_step', out_shape=(pltpu.VMEM((8, 128),...  50.9 us
    pallas_call x1, Pallas kernels, per_device(): pl.pallas_call(finish, name='finish', out_shape=(jax.ShapeDtypeStruct((1,...  1.27 us

profile of v6, /device:TPU:1, one launch (start us, length us, event | category | flops | bytes accessed | tf_op | source)
XLA Modules:
  0.0 52.8 jit_solution(2668485584301774067)
XLA Ops:
  0.6 50.9 %gibbs_step.1 = (f32[8,128]{1,0:T(8,128)S(1)}, f32[3,128,128]{2,1,0:T(8,128)S(1)}, f32[6,64,128]{2,1,0:T(8,128)S(1)}) custom-call(f32[128,256]{1,0:T(8,128)} %bitcast.15, s32[128,256]{1,0:T(8,128)} %bitcast.16, f32[128,256]{1,0:T(8,128)} %bitcast.17, s32[1,128]{1,0:T(1,128)} %bitcast.18, f32[3,128,128]{2,1,0:T(8,128)} %bitcast.14, f32[3,64,128]{2,1,0:T(8,128)} %prec.1, ...), custom_call_target="tpu_custom_call" | custom-call | tf_op jit(solution)/shard_map/gibbs_step/pallas_call | solution.py:594
  51.5 1.3 %finish.1 = (f32[1,1]{1,0:T(1,128)}, f32[3,128,128]{2,1,0:T(8,128)}, f32[6,64,128]{2,1,0:T(8,128)}) custom-call(f32[8,128]{1,0:T(8,128)S(1)} %get-tuple-element.9.small, f32[3,128,128]{2,1,0:T(8,128)S(1)} %get-tuple-element.10.map_in, f32[6,64,128]{2,1,0:T(8,128)S(1)} %get-tuple-element.11.sol_in), custom_call_target="tpu_custom_call" | custom-call | tf_op jit(solution)/shard_map/finish/pallas_call | solution.py:654

commit v7 on v6

--- a/solution.py
+++ b/solution.py
@@ -14,10 +14,10 @@
 NDET = 4
 NTM = 32
 NDEV = NDET * NTM
-GROUP = 16
+GROUP = 32
 NGROUP = NDEV // GROUP
-LOWER = 12
-UNROLL = 32
+LOWER = 24
+UNROLL = 64
 SHIFT = 4.0
 SCALE = 4.0
 STEP_MAX = 20.0
@@ -106,6 +106,33 @@
     tm = lax.axis_index("tm")
     me = det * NTM + tm
 
+    ty, tz, tc = tm // 8, (tm // 2) % 4, tm % 2
+    at_z = [(tz + o) % 4 * 2 for o in range(4)]
+    at_c = [tc, 1 - tc]
+    at_y = [(ty + o) % 4 * 8 for o in range(4)]
+    at_det = [(det + o) % NDET for o in range(NDET)]
+
+    def to_tm(act):
+        def row(y, own):
+            for z in (2, 1, 3, 0):
+                for c in (1, 0):
+                    if not (own and z == 0 and c == 0):
+                        act(y * 8 + at_z[z] + at_c[c])
+
+        @pl.loop(0, 3)
+        def _(d):
+            row((ty + jnp.where(d == 0, 2, jnp.where(d == 1, 1, 3))) % 4, False)
+
+        row(ty, True)
+
+    def to_all(act):
+        to_tm(lambda to: [act((at_det[x], to)) for x in (2, 1, 3, 0)])
+        for x in (2, 1, 3):
+            act((at_det[x], tm))
+
+    barrier = pltpu.get_barrier_semaphore()
+    to_all(lambda to: pl.semaphore_signal(barrier, inc=1, device_id=to, device_id_type=MESH))
+
     loads = [
         pltpu.make_async_copy(src, dst, in_sem.at[i])
         for i, (src, dst) in enumerate((
@@ -116,33 +143,6 @@
     ]
     for load in loads:
         load.start()
-
-    ty, tz, tc = tm // 8, (tm // 2) % 4, tm % 2
-    at_z = [(tz + o) % 4 * 2 for o in range(4)]
-    at_c = [tc, 1 - tc]
-    at_y = [(ty + o) % 4 * 8 for o in range(4)]
-    at_det = [(det + o) % NDET for o in range(NDET)]
-
-    def to_tm(act):
-        def row(y, own):
-            for z in (2, 1, 3, 0):
-                for c in (1, 0):
-                    if not (own and z == 0 and c == 0):
-                        act(y * 8 + at_z[z] + at_c[c])
-
-        @pl.loop(0, 3)
-        def _(d):
-            row((ty + jnp.where(d == 0, 2, jnp.where(d == 1, 1, 3))) % 4, False)
-
-        row(ty, True)
-
-    def to_all(act):
-        to_tm(lambda to: [act((at_det[x], to)) for x in (2, 1, 3, 0)])
-        for x in (2, 1, 3):
-            act((at_det[x], tm))
-
-    barrier = pltpu.get_barrier_semaphore()
-    to_all(lambda to: pl.semaphore_signal(barrier, inc=1, device_id=to, device_id_type=MESH))
 
     for load in loads[:4]:
         load.wait()
@@ -251,19 +251,22 @@
             upper = (pixel >> 13) * 128 + ((pixel >> 6) & 1) * 64 + ((pixel >> 7) & 63)
             hi_s[half, here, :] = upper.astype(F32)
             lo_s[half, here, :] = (pixel & 63).astype(F32)
-        pixel = jnp.concatenate(
-            [rbuf[pl.ds((base + LOWER) * 8 + 4 + half, GROUP - LOWER, stride=8), :] for half in range(2)], axis=0
-        ).astype(jnp.int32)
-        in_row, at_lane = ((pixel >> 7) & 63) * 2 + (pixel >> 13), pixel & 127
-        picked = [jnp.zeros((8, 128), F32) for _ in range(3)]
-
-        def permute_rows(first_r, last_r):
-            for r in range(first_r, last_r):
+        picked = {}
+        places = {}
+
+        def permute_rows(first_step, last_step):
+            for step in range(first_step, last_step):
+                half, r = divmod(step, 128)
+                if r == 0:
+                    pixel = rbuf[pl.ds((base + LOWER) * 8 + 4 + half, GROUP - LOWER, stride=8), :].astype(jnp.int32)
+                    places[half] = (((pixel >> 7) & 63) * 2 + (pixel >> 13), pixel & 127)
+                    picked[half] = [jnp.zeros((GROUP - LOWER, 128), F32) for _ in range(3)]
+                in_row, at_lane = places[half]
                 same = in_row == r
                 for c in range(3):
-                    line = jnp.broadcast_to(sky[c, r : r + 1, :], (8, 128))
+                    line = jnp.broadcast_to(sky[c, r : r + 1, :], (GROUP - LOWER, 128))
                     taken = jnp.take_along_axis(line, at_lane, axis=1)
-                    picked[c] = jnp.where(same, taken, picked[c])
+                    picked[half][c] = jnp.where(same, taken, picked[half][c])
 
         for u in range(LOWER):
             s = base + u
@@ -278,10 +281,10 @@
                     look[c, half, pl.ds(s, 1), :] = jnp.sum(
                         jnp.where(same, part, 0.0), axis=0, keepdims=True
                     )
-            permute_rows(u * 128 // LOWER, (u + 1) * 128 // LOWER)
+            permute_rows(u * 256 // LOWER, (u + 1) * 256 // LOWER)
         for half in range(2):
             for c in range(3):
-                look[c, half, pl.ds(base + LOWER, GROUP - LOWER), :] = picked[c][half * 4 : half * 4 + 4]
+                look[c, half, pl.ds(base + LOWER, GROUP - LOWER), :] = picked[half][c]
         count = row(6)
         cross = jnp.zeros((GROUP, 128), F32)
         square = jnp.zeros((GROUP, 128), F32)
@@ -572,14 +575,15 @@
             copy.wait_send()
 
 
-def finish(small, map_in, sol_in, gain_out, map_out, sol_out, out_sem):
+def finish(small, map_in, sol_in, gain_out, map_out, sol_out, gain, out_sem):
+    gain[...] = small[0:1, 0:1]
     stores = [
         pltpu.make_async_copy(sol_in, sol_out, out_sem.at[0]),
         pltpu.make_async_copy(map_in, map_out, out_sem.at[1]),
+        pltpu.make_async_copy(gain, gain_out, out_sem.at[2]),
     ]
     for store in stores:
         store.start()
-    gain_out[...] = small[0:1, 0:1]
     for store in stores:
         store.wait()
 
@@ -660,8 +664,8 @@
             jax.ShapeDtypeStruct((6, 64, 128), F32),
         ),
         in_specs=[vmem, vmem, vmem],
-        out_specs=(vmem, anywhere, anywhere),
-        scratch_shapes=[dma((2,))],
+        out_specs=(anywhere, anywhere, anywhere),
+        scratch_shapes=[pltpu.VMEM((1, 1), F32), dma((3,))],
     )(*(pltpu.with_memory_space_constraint(x, pltpu.VMEM) for x in (small, binned, solved)))
     binned = binned.reshape(3, 64, 2, 128).transpose(0, 2, 1, 3).reshape(3, 2, 8192)
     return (gain, binned, solved)

time: 52.9 us -> 52.6 us (level)
  no operation moved by 1% of the time
where the time goes in v7:
time: 52.6 us; the launch traced here: 52.5 us
  Pallas kernels  51.8 us (98%)
  between operations  0.64 us (1%)
    pallas_call x1, Pallas kernels, per_device(): pl.pallas_call(kernel, name='gibbs_step', out_shape=(pltpu.VMEM((8, 128),...  51 us

profile of v7, /device:TPU:1, one launch (start us, length us, event | category | flops | bytes accessed | tf_op | source)
XLA Modules:
  0.0 52.5 jit_solution(4814166597404458797)
XLA Ops:
  0.6 51.0 %gibbs_step.1 = (f32[8,128]{1,0:T(8,128)S(1)}, f32[3,128,128]{2,1,0:T(8,128)S(1)}, f32[6,64,128]{2,1,0:T(8,128)S(1)}) custom-call(f32[128,256]{1,0:T(8,128)} %bitcast.15, s32[128,256]{1,0:T(8,128)} %bitcast.16, f32[128,256]{1,0:T(8,128)} %bitcast.17, s32[1,128]{1,0:T(1,128)} %bitcast.18, f32[3,128,128]{2,1,0:T(8,128)} %bitcast.14, f32[3,64,128]{2,1,0:T(8,128)} %prec.1, ...), custom_call_target="tpu_custom_call" | custom-call | tf_op jit(solution)/shard_map/gibbs_step/pallas_call | solution.py:598
  51.7 0.8 %finish.1 = (f32[1,1]{1,0:T(1,128)}, f32[3,128,128]{2,1,0:T(8,128)}, f32[6,64,128]{2,1,0:T(8,128)}) custom-call(f32[8,128]{1,0:T(8,128)S(1)} %get-tuple-element.9.small, f32[3,128,128]{2,1,0:T(8,128)S(1)} %get-tuple-element.10.map_in, f32[6,64,128]{2,1,0:T(8,128)S(1)} %get-tuple-element.11.sol_in), custom_call_target="tpu_custom_call" | custom-call | tf_op jit(solution)/shard_map/finish/pallas_call | solution.py:658

commit v8 on v7

--- a/solution.py
+++ b/solution.py
@@ -14,9 +14,9 @@
 NDET = 4
 NTM = 32
 NDEV = NDET * NTM
-GROUP = 32
+GROUP = 16
 NGROUP = NDEV // GROUP
-LOWER = 24
+LOWER = 12
 UNROLL = 64
 SHIFT = 4.0
 SCALE = 4.0
@@ -251,22 +251,19 @@
             upper = (pixel >> 13) * 128 + ((pixel >> 6) & 1) * 64 + ((pixel >> 7) & 63)
             hi_s[half, here, :] = upper.astype(F32)
             lo_s[half, here, :] = (pixel & 63).astype(F32)
-        picked = {}
-        places = {}
-
-        def permute_rows(first_step, last_step):
-            for step in range(first_step, last_step):
-                half, r = divmod(step, 128)
-                if r == 0:
-                    pixel = rbuf[pl.ds((base + LOWER) * 8 + 4 + half, GROUP - LOWER, stride=8), :].astype(jnp.int32)
-                    places[half] = (((pixel >> 7) & 63) * 2 + (pixel >> 13), pixel & 127)
-                    picked[half] = [jnp.zeros((GROUP - LOWER, 128), F32) for _ in range(3)]
-                in_row, at_lane = places[half]
+        pixel = jnp.concatenate(
+            [rbuf[pl.ds((base + LOWER) * 8 + 4 + half, GROUP - LOWER, stride=8), :] for half in range(2)], axis=0
+        ).astype(jnp.int32)
+        in_row, at_lane = ((pixel >> 7) & 63) * 2 + (pixel >> 13), pixel & 127
+        picked = [jnp.zeros((8, 128), F32) for _ in range(3)]
+
+        def permute_rows(first_r, last_r):
+            for r in range(first_r, last_r):
                 same = in_row == r
                 for c in range(3):
-                    line = jnp.broadcast_to(sky[c, r : r + 1, :], (GROUP - LOWER, 128))
+                    line = jnp.broadcast_to(sky[c, r : r + 1, :], (8, 128))
                     taken = jnp.take_along_axis(line, at_lane, axis=1)
-                    picked[half][c] = jnp.where(same, taken, picked[half][c])
+                    picked[c] = jnp.where(same, taken, picked[c])
 
         for u in range(LOWER):
             s = base + u
@@ -281,10 +278,10 @@
                     look[c, half, pl.ds(s, 1), :] = jnp.sum(
                         jnp.where(same, part, 0.0), axis=0, keepdims=True
                     )
-            permute_rows(u * 256 // LOWER, (u + 1) * 256 // LOWER)
+            permute_rows(u * 128 // LOWER, (u + 1) * 128 // LOWER)
         for half in range(2):
             for c in range(3):
-                look[c, half, pl.ds(base + LOWER, GROUP - LOWER), :] = picked[half][c]
+                look[c, half, pl.ds(base + LOWER, GROUP - LOWER), :] = picked[c][half * 4 : half * 4 + 4]
         count = row(6)
         cross = jnp.zeros((GROUP, 128), F32)
         square = jnp.zeros((GROUP, 128), F32)

time: 52.6 us -> 52 us (0.989)
  Pallas kernels: 51.8 us -> 51.2 us
    pallas_call x1, Pallas kernels: 51 us -> 50.5 us  [per_device(): pl.pallas_call(kernel, name='gibbs_step', out_shape=(pltpu.VMEM((8, 128),...]
where the time goes in v8:
time: 52 us; the launch traced here: 51.9 us
  Pallas kernels  51.2 us (98%)
  between operations  0.64 us (1%)
    pallas_call x1, Pallas kernels, per_device(): pl.pallas_call(kernel, name='gibbs_step', out_shape=(pltpu.VMEM((8, 128),...  50.5 us

profile of v8, /device:TPU:1, one launch (start us, length us, event | category | flops | bytes accessed | tf_op | source)
XLA Modules:
  0.0 51.9 jit_solution(13747200012061392296)
XLA Ops:
  0.6 50.5 %gibbs_step.1 = (f32[8,128]{1,0:T(8,128)S(1)}, f32[3,128,128]{2,1,0:T(8,128)S(1)}, f32[6,64,128]{2,1,0:T(8,128)S(1)}) custom-call(f32[128,256]{1,0:T(8,128)} %bitcast.15, s32[128,256]{1,0:T(8,128)} %bitcast.16, f32[128,256]{1,0:T(8,128)} %bitcast.17, s32[1,128]{1,0:T(1,128)} %bitcast.18, f32[3,128,128]{2,1,0:T(8,128)} %bitcast.14, f32[3,64,128]{2,1,0:T(8,128)} %prec.1, ...), custom_call_target="tpu_custom_call" | custom-call | tf_op jit(solution)/shard_map/gibbs_step/pallas_call | solution.py:595
  51.1 0.8 %finish.1 = (f32[1,1]{1,0:T(1,128)}, f32[3,128,128]{2,1,0:T(8,128)}, f32[6,64,128]{2,1,0:T(8,128)}) custom-call(f32[8,128]{1,0:T(8,128)S(1)} %get-tuple-element.9.small, f32[3,128,128]{2,1,0:T(8,128)S(1)} %get-tuple-element.10.map_in, f32[6,64,128]{2,1,0:T(8,128)S(1)} %get-tuple-element.11.sol_in), custom_call_target="tpu_custom_call" | custom-call | tf_op jit(solution)/shard_map/finish/pallas_call | solution.py:655

commit v9 on v8

--- a/solution.py
+++ b/solution.py
@@ -318,7 +318,7 @@
         )
         for k in range(2)
     )
-    mine = stat_r.at[me]
+    mine = stat_r.at[me // 4, pl.ds(me % 4 * 2, 2), :]
     mine[...] = jnp.concatenate([cross, square], axis=0)
     to_all(
         lambda to: pltpu.make_async_remote_copy(
@@ -339,9 +339,10 @@
         valid = jnp.where(good, 1.0, 0.0)
         hits[1] = hits[1] + jnp.sum(valid * late, axis=0, keepdims=True)
         hits[0] = hits[0] + jnp.sum(valid * (1.0 - late), axis=0, keepdims=True)
-    rest = stat_r.at[pl.ds(0, NDEV - 1)]
+    rest = sbuf.at[pl.ds(0, 2 * (NDEV - 1))]
     pltpu.make_async_copy(rest, rest, stat_recv).wait()
     total = jnp.sum(stat_r[...], axis=0)
+    total = total[0:2] + total[2:4] + total[4:6] + total[6:8]
     gains = total[0:1] / (total[1:2] + 1e-06)
     lane = lax.broadcasted_iota(jnp.int32, (1, 128), 1)
     own_gain = jnp.sum(jnp.where(lane == me, gains, 0.0), axis=1, keepdims=True)
@@ -497,16 +498,16 @@
     for m in range(6):
         value = jnp.sum(jnp.sum(moments[m], axis=0, keepdims=True), axis=1, keepdims=True)
         message = jnp.where(lane == m, jnp.broadcast_to(value, (1, 128)), message)
-    own_row = mom_r.at[me]
+    own_row = mom_r.at[me // 8, pl.ds(me % 8, 1), :]
     own_row[...] = message
     to_all(
         lambda to: pltpu.make_async_remote_copy(
             own_row, own_row, mom_send, mom_recv, device_id=to, device_id_type=MESH
         ).start()
     )
-    rest = mom_r.at[pl.ds(0, NDEV - 1)]
+    rest = sbuf.at[pl.ds(0, NDEV - 1)]
     pltpu.make_async_copy(rest, rest, mom_recv).wait()
-    sums = jnp.sum(mom_r[...], axis=0)
+    sums = jnp.sum(jnp.sum(mom_r[...], axis=0), axis=0, keepdims=True)
     nu = [jnp.sum(jnp.where(lane == m, sums, 0.0), axis=1, keepdims=True) for m in range(6)]
 
     zero = jnp.zeros((1, 1), F32)
@@ -548,11 +549,11 @@
 
     span = sbuf.at[pl.ds(0, (NDEV - 1) * 8)]
     pltpu.make_async_copy(span, span, send_sem).wait()
-    rest = stat_r.at[pl.ds(0, NDEV - 1)]
+    rest = sbuf.at[pl.ds(0, 2 * (NDEV - 1))]
     pltpu.make_async_copy(rest, rest, stat_send).wait()
     span = spec_s.at[pl.ds(0, (NTM - 1) * 16)]
     pltpu.make_async_copy(span, span, spec_send).wait()
-    rest = mom_r.at[pl.ds(0, NDEV - 1)]
+    rest = sbuf.at[pl.ds(0, NDEV - 1)]
     pltpu.make_async_copy(rest, rest, mom_send).wait()
 
     for here, tiles in rims:
@@ -626,7 +627,7 @@
             pltpu.VMEM((2, 128, 128), F32),
             pltpu.VMEM((6, 2, 128, 128), F32),
             pltpu.VMEM((384, 256), F32),
-            pltpu.VMEM((NDEV, 2, 128), F32),
+            pltpu.VMEM((NDEV // 4, 8, 128), F32),
             pltpu.VMEM((NTM * 16, 128), F32),
             pltpu.VMEM((70 * 8, 128), F32),
             pltpu.VMEM((3, 80, 128), F32),
@@ -635,7 +636,7 @@
             pltpu.VMEM((7, 80, 128), F32),
             pltpu.VMEM((6, 64, 128), F32),
             pltpu.VMEM((6, 64, 128), F32),
-            pltpu.VMEM((NDEV, 1, 128), F32),
+            pltpu.VMEM((NDEV // 8, 8, 128), F32),
             dma, dma((NGROUP,)), dma, dma, dma, dma,
             dma, dma((2,)), dma((2, 3)), dma((2, 3)), dma, dma,
             dma((12,)),

time: 52 us -> 51.8 us (level)
  no operation moved by 1% of the time
where the time goes in v9:
time: 51.8 us; the launch traced here: 51.7 us
  Pallas kernels  51 us (98%)
  between operations  0.64 us (1%)
    pallas_call x1, Pallas kernels, per_device(): pl.pallas_call(kernel, name='gibbs_step', out_shape=(pltpu.VMEM((8, 128),...  50.3 us

profile of v9, /device:TPU:1, one launch (start us, length us, event | category | flops | bytes accessed | tf_op | source)
XLA Modules:
  0.0 51.7 jit_solution(6130118449026550552)
XLA Ops:
  0.6 50.3 %gibbs_step.1 = (f32[8,128]{1,0:T(8,128)S(1)}, f32[3,128,128]{2,1,0:T(8,128)S(1)}, f32[6,64,128]{2,1,0:T(8,128)S(1)}) custom-call(f32[128,256]{1,0:T(8,128)} %bitcast.15, s32[128,256]{1,0:T(8,128)} %bitcast.16, f32[128,256]{1,0:T(8,128)} %bitcast.17, s32[1,128]{1,0:T(1,128)} %bitcast.18, f32[3,128,128]{2,1,0:T(8,128)} %bitcast.14, f32[3,64,128]{2,1,0:T(8,128)} %prec.1, ...), custom_call_target="tpu_custom_call" | custom-call | tf_op jit(solution)/shard_map/gibbs_step/pallas_call | solution.py:596
  50.9 0.8 %finish.1 = (f32[1,1]{1,0:T(1,128)}, f32[3,128,128]{2,1,0:T(8,128)}, f32[6,64,128]{2,1,0:T(8,128)}) custom-call(f32[8,128]{1,0:T(8,128)S(1)} %get-tuple-element.9.small, f32[3,128,128]{2,1,0:T(8,128)S(1)} %get-tuple-element.10.map_in, f32[6,64,128]{2,1,0:T(8,128)S(1)} %get-tuple-element.11.sol_in), custom_call_target="tpu_custom_call" | custom-call | tf_op jit(solution)/shard_map/finish/pallas_call | solution.py:656

commit v10 on v9

--- a/solution.py
+++ b/solution.py
@@ -17,7 +17,7 @@
 GROUP = 16
 NGROUP = NDEV // GROUP
 LOWER = 12
-UNROLL = 64
+UNROLL = 128
 SHIFT = 4.0
 SCALE = 4.0
 STEP_MAX = 20.0

time: 51.8 us -> 51.8 us (level)
  no operation moved by 1% of the time
where the time goes in v10:
time: 51.8 us; the launch traced here: 51.7 us
  Pallas kernels  51.1 us (99%)
  between operations  0.64 us (1%)
    pallas_call x1, Pallas kernels, per_device(): pl.pallas_call(kernel, name='gibbs_step', out_shape=(pltpu.VMEM((8, 128),...  50.3 us

profile of v10, /device:TPU:1, one launch (start us, length us, event | category | flops | bytes accessed | tf_op | source)
XLA Modules:
  0.0 51.7 jit_solution(5474573289733286658)
XLA Ops:
  0.6 50.3 %gibbs_step.1 = (f32[8,128]{1,0:T(8,128)S(1)}, f32[3,128,128]{2,1,0:T(8,128)S(1)}, f32[6,64,128]{2,1,0:T(8,128)S(1)}) custom-call(f32[128,256]{1,0:T(8,128)} %bitcast.15, s32[128,256]{1,0:T(8,128)} %bitcast.16, f32[128,256]{1,0:T(8,128)} %bitcast.17, s32[1,128]{1,0:T(1,128)} %bitcast.18, f32[3,128,128]{2,1,0:T(8,128)} %bitcast.14, f32[3,64,128]{2,1,0:T(8,128)} %prec.1, ...), custom_call_target="tpu_custom_call" | custom-call | tf_op jit(solution)/shard_map/gibbs_step/pallas_call | solution.py:596
  50.9 0.8 %finish.1 = (f32[1,1]{1,0:T(1,128)}, f32[3,128,128]{2,1,0:T(8,128)}, f32[6,64,128]{2,1,0:T(8,128)}) custom-call(f32[8,128]{1,0:T(8,128)S(1)} %get-tuple-element.9.small, f32[3,128,128]{2,1,0:T(8,128)S(1)} %get-tuple-element.10.map_in, f32[6,64,128]{2,1,0:T(8,128)S(1)} %get-tuple-element.11.sol_in), custom_call_target="tpu_custom_call" | custom-call | tf_op jit(solution)/shard_map/finish/pallas_call | solution.py:656

commit v11 on v10

--- a/solution.py
+++ b/solution.py
@@ -192,7 +192,6 @@
     source = ((code & 3) + det) % 4 * 32 + (((code >> 2) & 3) + ty) % 4 * 8
     source = source + (((code >> 4) & 3) + tz) % 4 * 2 + ((code >> 6) + tc) % 2
     match_s[...] = jnp.where(source == col_i, 1.0, 0.0)
-    acc[...] = jnp.zeros_like(acc)
     pl.semaphore_wait(barrier, NDEV - 1)
 
     for s, (x, y, z, c) in enumerate(NEAR):
@@ -373,7 +372,7 @@
                     value = jnp.broadcast_to(wsplit[w, half, pl.ds(s, 1), :], (16, 128)).astype(BF16)
                     rows.append(jnp.where(same, value[None], jnp.zeros((), BF16)).reshape(64, 128))
                 lefts.append(jnp.concatenate(rows, axis=0))
-        acc[...] += lax.dot_general(
+        acc[...] = lax.dot_general(
             jnp.concatenate(lefts, axis=1), jnp.concatenate(rights, axis=1),
             (((1,), (1,)), ((), ())), preferred_element_type=F32,
         )

time: 51.8 us -> 51.8 us (level)
  no operation moved by 1% of the time
where the time goes in v11:
time: 51.8 us; the launch traced here: 51.7 us
  Pallas kernels  51.1 us (99%)
  between operations  0.64 us (1%)
    pallas_call x1, Pallas kernels, per_device(): pl.pallas_call(kernel, name='gibbs_step', out_shape=(pltpu.VMEM((8, 128),...  50.3 us

profile of v11, /device:TPU:1, one launch (start us, length us, event | category | flops | bytes accessed | tf_op | source)
XLA Modules:
  0.0 51.7 jit_solution(2478769086861068183)
XLA Ops:
  0.6 50.3 %gibbs_step.1 = (f32[8,128]{1,0:T(8,128)S(1)}, f32[3,128,128]{2,1,0:T(8,128)S(1)}, f32[6,64,128]{2,1,0:T(8,128)S(1)}) custom-call(f32[128,256]{1,0:T(8,128)} %bitcast.15, s32[128,256]{1,0:T(8,128)} %bitcast.16, f32[128,256]{1,0:T(8,128)} %bitcast.17, s32[1,128]{1,0:T(1,128)} %bitcast.18, f32[3,128,128]{2,1,0:T(8,128)} %bitcast.14, f32[3,64,128]{2,1,0:T(8,128)} %prec.1, ...), custom_call_target="tpu_custom_call" | custom-call | tf_op jit(solution)/shard_map/gibbs_step/pallas_call | solution.py:595
  50.9 0.8 %finish.1 = (f32[1,1]{1,0:T(1,128)}, f32[3,128,128]{2,1,0:T(8,128)}, f32[6,64,128]{2,1,0:T(8,128)}) custom-call(f32[8,128]{1,0:T(8,128)S(1)} %get-tuple-element.9.small, f32[3,128,128]{2,1,0:T(8,128)S(1)} %get-tuple-element.10.map_in, f32[6,64,128]{2,1,0:T(8,128)S(1)} %get-tuple-element.11.sol_in), custom_call_target="tpu_custom_call" | custom-call | tf_op jit(solution)/shard_map/finish/pallas_call | solution.py:655
